TPU v7x, 128 devices: a whole 4x4x4 slice. The times are simulated.
128 devices in a mesh: ctx: 16 (over x, y), head: 8 (over z, core).
Axes of the slice: x: 4, y: 4, z: 4, core: 2. Of those that a mesh axis runs over, the one named last changes fastest.
Arguments:
- queries: bfloat16 [4, 6144, 6144], P(None, 'ctx', 'head'), may hold values from -6 to 6
- keys_values: bfloat16 [4, 6144, 3072], P(None, 'ctx', 'head'), may hold values from -25 to 25
- block_lists: int32 [4, 48, 16], P(None, 'ctx'), may hold values from -1 to 47, as said below
- starts: int32 [4], replicated, may hold values from 0 to 3071, as said below
- norm_gain: bfloat16 [6144], P('head'), may hold values from 0.5 to 1.5
Outputs:
- mixed_out: bfloat16 [4, 6144, 6144], P(None, 'ctx', 'head')
Inputs may be any that keep to these rules, and one draw needn't show every extreme that they name: `block_lists`: entry [b, j, s] is a block of 128 positions of prompt b, or -1 for an unused slot. The entries of one list are distinct blocks from the prompt's first block (the block holding starts[b]) up to j, always including that first block and j itself; a list is all -1 where j lies before the first block. For each prompt, the lists of the query blocks held by one index of ctx name at most one block held by any other index of ctx, and this bound is reached. One prompt starts at 0 and one at 3071.
All inputs are finite; a program needn't handle non-finite values.
Results may differ from a plain program's by a relative error of at most 0.0041.
Values may be sent and summed in bfloat16 or wider, within the bound.
A program may use at most 128 MiB of HBM per device.

v0:
```python
import math

import jax
import jax.numpy as jnp
from jax import lax
from jax.sharding import PartitionSpec as P

HD = 96
BLK = 128
TOPK = 16


epsilon = 1e-06
masked_score = -1e30


def prefix(shard, axis, combine, identity):
    count, mine = (lax.axis_size(axis), lax.axis_index(axis))
    everything = jax.tree.map(
        lambda part, kind: lax.all_gather(part.astype(kind), axis),
        shard,
        (jnp.bfloat16, jnp.bfloat16),
    )
    start = jax.tree.map(
        lambda part, zero: jnp.broadcast_to(jnp.asarray(zero, part.dtype), part.shape),
        shard,
        identity,
    )

    def step(k, before):
        reached = k < mine
        new = combine(
            before, jax.tree.map(lambda part, own: part[k].astype(own.dtype), everything, shard)
        )
        return jax.tree.map(lambda a, b: jnp.where(reached, a, b), new, before)

    return lax.fori_loop(0, count, step, start)


def feature_map(values):
    return jax.nn.elu(values) + 1.0


def add_states(earlier, later):
    return (earlier[0] + later[0], earlier[1] + later[1])


def on_device(queries, keys_values, block_lists, starts, norm_gain):
    seq_count, local_len, feature_count = queries.shape
    kv_width = keys_values.shape[2]
    kv_local = kv_width // (2 * HD)
    group_size = feature_count // HD // kv_local
    stretch_count = local_len // BLK
    ctx_rank = lax.axis_index("ctx")
    highest = lax.Precision.HIGHEST
    positions = ctx_rank * local_len + jnp.arange(local_len, dtype=jnp.int32)
    usable = positions[None, :] >= starts[:, None]
    usable_stretches = usable.reshape(seq_count, stretch_count, BLK)
    query_stretches = queries.reshape(seq_count, stretch_count, BLK, kv_local, group_size, HD)
    kv_stretches = keys_values.reshape(seq_count, stretch_count, BLK, kv_local, 2, HD)
    value_stretches = kv_stretches[:, :, :, :, 1, :]
    phi_query = lax.optimization_barrier(
        feature_map(query_stretches.astype(jnp.float32)).astype(jnp.bfloat16)
    )
    phi_key = (
        feature_map(kv_stretches[:, :, :, :, 0, :].astype(jnp.float32))
        * usable_stretches[:, :, :, None, None]
    ).astype(jnp.bfloat16)
    stretch_states = jnp.einsum(
        "bctgd,bctge->bcgde", phi_key, value_stretches, preferred_element_type=jnp.float32
    )
    stretch_normals = jnp.sum(phi_key.astype(jnp.float32), axis=2)
    device_state = jnp.sum(stretch_states, axis=1)
    device_normal = jnp.sum(stretch_normals, axis=1)
    identity = (jnp.zeros_like(device_state), jnp.zeros_like(device_normal))
    prior_state, prior_normal = prefix((device_state, device_normal), "ctx", add_states, identity)
    running_state = prior_state[:, None] + jnp.cumsum(stretch_states, axis=1) - stretch_states
    running_normal = prior_normal[:, None] + jnp.cumsum(stretch_normals, axis=1) - stretch_normals
    causal = jnp.arange(BLK)[:, None] >= jnp.arange(BLK)[None, :]
    inner_scores = jnp.einsum(
        "bctgxd,bcsgd->bcgxts", phi_query, phi_key, preferred_element_type=jnp.float32
    )
    inner_scores = jnp.where(causal, inner_scores, 0.0)
    inner_sum = jnp.transpose(jnp.sum(inner_scores, axis=-1), (0, 1, 4, 2, 3))
    inner_num = jnp.einsum(
        "bcgxts,bcsge->bctgxe",
        inner_scores.astype(jnp.bfloat16),
        value_stretches,
        preferred_element_type=jnp.float32,
    )
    query_float = phi_query.astype(jnp.float32)
    state_num = jnp.einsum("bctgxd,bcgde->bctgxe", query_float, running_state, precision=highest)
    state_den = jnp.einsum("bctgxd,bcgd->bctgx", query_float, running_normal, precision=highest)
    row_usable = usable_stretches[:, :, :, None, None]
    denominator = jnp.where(row_usable, inner_sum + state_den, 1.0)
    linear_out = jnp.where(
        row_usable[..., None], (inner_num + state_num) / denominator[..., None], 0.0
    )
    linear_out = linear_out.reshape(seq_count, local_len, feature_count)
    kv_blocks = keys_values.reshape(seq_count, stretch_count, BLK, kv_width)
    candidates = lax.all_gather(kv_blocks, "ctx", axis=1, tiled=True)
    slot_ids = jnp.maximum(block_lists, 0)
    offsets = jnp.arange(BLK, dtype=jnp.int32)
    score_scale = 1.0 / math.sqrt(HD)
    query_rows = positions.reshape(stretch_count, BLK)

    def attend(number):
        seq_index = number // stretch_count
        stretch_index = number % stretch_count
        query_block = lax.dynamic_index_in_dim(
            lax.dynamic_index_in_dim(query_stretches, seq_index, 0, False), stretch_index, 0, False
        )
        seq_pool = lax.dynamic_index_in_dim(candidates, seq_index, 0, False)
        chosen = lax.dynamic_index_in_dim(
            lax.dynamic_index_in_dim(block_lists, seq_index, 0, False), stretch_index, 0, False
        )
        block_slots = lax.dynamic_index_in_dim(
            lax.dynamic_index_in_dim(slot_ids, seq_index, 0, False), stretch_index, 0, False
        )
        picked = jnp.take(seq_pool, block_slots, axis=0).reshape(TOPK * BLK, kv_local, 2, HD)
        key_pos = (jnp.maximum(chosen, 0)[:, None] * BLK + offsets[None, :]).reshape(TOPK * BLK)
        listed = jnp.repeat(chosen >= 0, BLK)
        query_pos = lax.dynamic_index_in_dim(query_rows, stretch_index, 0, False)
        first_live = lax.dynamic_index_in_dim(starts, seq_index, 0, False)
        allowed = (
            listed[None, :]
            & (key_pos[None, :] <= query_pos[:, None])
            & (key_pos[None, :] >= first_live)
        )
        scores = (
            jnp.einsum(
                "xghd,kgd->ghxk",
                query_block,
                picked[:, :, 0, :],
                preferred_element_type=jnp.float32,
            )
            * score_scale
        )
        scores = jnp.where(allowed[None, None], scores, masked_score)
        top_score = jnp.max(scores, axis=-1, keepdims=True)
        weights = jnp.where(allowed[None, None], jnp.exp(scores - top_score), 0.0)
        weight_sum = jnp.transpose(jnp.sum(weights, axis=-1), (2, 0, 1))
        gathered = jnp.einsum(
            "ghxk,kge->xghe",
            weights.astype(jnp.bfloat16),
            picked[:, :, 1, :],
            preferred_element_type=jnp.float32,
        )
        row_ok = (query_pos >= first_live)[:, None, None]
        result = jnp.where(
            row_ok[..., None], gathered / jnp.where(row_ok, weight_sum, 1.0)[..., None], 0.0
        )
        return result.reshape(BLK, feature_count)

    sparse_parts = lax.map(attend, jnp.arange(seq_count * stretch_count, dtype=jnp.int32))
    sparse_out = sparse_parts.reshape(seq_count, local_len, feature_count)
    combined = linear_out + sparse_out
    squares = jnp.sum(combined * combined, axis=-1)
    all_squares = lax.psum(squares, "head")
    full_width = feature_count * lax.axis_size("head")
    scaled = (
        combined
        * lax.rsqrt(all_squares / full_width + epsilon)[..., None]
        * norm_gain.astype(jnp.float32)
    )
    return scaled.astype(jnp.bfloat16)


def solution(mesh):
    return jax.shard_map(
        on_device,
        mesh=mesh,
        in_specs=(
            P(None, "ctx", "head"),
            P(None, "ctx", "head"),
            P(None, "ctx", None),
            P(),
            P("head"),
        ),
        out_specs=P(None, "ctx", "head"),
        check_vma=False,
    )
```

profile of v0, /device:TPU:1, one launch (start us, length us, event | category | flops | bytes accessed | tf_op | source)
XLA Modules:
  0.0 764.1 jit_solution(8744335096811571887)
XLA Ops:
  23.0 6.5 reshape.308
  38.2 19.4 %all-gather.1 = bf16[64,2,96]{2,1,0:T(2,128)(2,1)S(1)} all-gather(bf16[4,2,96]{2,1,0:T(2,128)(2,1)S(1)} %fusion.66), channel_id=3, replica_groups=mesh['ctx'=16,'head'=8] {'ctx'}, dimensions={0}, use_global_device_ids=true | all-gather | bytes 26112 | tf_op jit(solution)/shard_map/all_gather | solution.py:20
  63.6 9.5 %all-gather.7.cloned.1.call-done = bf16[64,2,96,96]{3,2,1,0:T(8,128)(2,1)} async-done(((bf16[4,2,96,96]{3,2,1,0:T(8,128)(2,1)}), bf16[64,2,96,96]{3,2,1,0:T(8,128)(2,1)}) %all-gather.7.cloned.1.call-update) | async-done | bytes 2359312 | tf_op jit(solution)/shard_map/all_gather | solution.py:20
  73.2 19.0 %while.31 = (s32[]{:T(128)}, f32[4,2,96,96]{3,2,1,0:T(8,128)S(1)}, f32[4,2,96]{2,1,0:T(2,128)S(1)}, s32[]{:T(128)}, bf16[16,4,2,96,96]{4,3,2,1,0:T(8,128)(2,1)},...) while((s32[]{:T(128)}, f32[4,2,96,96]{3,2,1,0:T(8,128)S(1)}, ...), condition=%wide.region_3.4_spmd.clone, body=%wide.region_2.3_spmd.clone.sunk | while | flops 297988 | bytes 745083 | solution.py:37
  94.2 102.3 %all-gather.5.cloned.1.call-done = bf16[4,48,128,384]{3,2,1,0:T(8,128)(2,1)} async-done(((bf16[4,3,128,384]{3,2,1,0:T(8,128)(2,1)}), bf16[4,48,128,384]{3,2,1,0:T(8,128)(2,1)}) %all-gather.5.cloned.1.call-update) | async-done | bytes 18874384 | tf_op jit(solution)/shard_map/all_gather | solution.py:101
  197.0 511.6 %while.30 = (s32[]{:T(128)}, f32[12,128,768]{1,2,0:T(8,128)}, s32[12]{0:T(128)}, s32[3,128]{1,0:T(4,128)S(1)}, s32[4]{0:T(128)S(1)}, /*index=5*/s32[4,3,16]{2,1,...) while((s32[]{:T(128)}, f32[12,128,768]{1,2,0:T(8,128)}, ...), condition=%wide.region_11.12_spmd.clone, body=%wide.region_8.11_spmd.clone.sunk | while | flops 819669376 | bytes 34196880 | solution.py:155
  215.6 6.3 reshape.344
  228.8 7.2 fusion.98
  258.3 6.3 reshape.344
  271.5 7.2 fusion.98
  314.2 7.2 fusion.98
  356.8 7.2 fusion.98
  399.4 7.2 fusion.98
  442.1 7.2 fusion.98
  484.8 7.2 fusion.98
  527.5 7.2 fusion.98
  570.2 7.2 fusion.98
  612.7 7.2 fusion.98
  655.1 7.2 fusion.98
  697.6 7.2 fusion.98
  714.8 8.8 %multiply_reduce_fusion = (f32[4,3,128]{2,1,0:T(4,128)S(1)}, f32[4,3,128,2,4,96]{2,5,4,3,1,0:T(8,128)}) fusion(f32[4,3,128,2,4,96]{2,5,4,3,1,0:T(8,128)} %bitcast.223, f32[4,3,128,2,4]{2,4,3,1,0:T(4,128)} %fusion.64, f32[4,3,2,96,96,1]{4,3,5,2,1,0:T(8,128)S(1)} %fusion.53, bf16[4,3,128,2,4,96]{2,5,4,3,1,0:T(8,128)(2,1)S(1)} %copy-done.1, ...), kind=kOutput, calls=%fused_computation.65 | convolution fusion | flops 1366030848 | bytes 17456640 | tf_op jit(solution)/shard_map/bctgxd,bcgde->bctgxe/dot_general | solution.py:92
  723.6 7.1 copy.61
  730.7 7.9 %reshape.309 = f32[4,384,768]{2,1,0:T(8,128)} reshape(f32[4,3,128,2,4,96]{5,4,3,2,1,0:T(4,128)} %copy.61) | data formatting | bytes 9437184 | tf_op jit(solution)/shard_map/reshape | solution.py:99
  738.7 12.7 %psum.7 = f32[4,384]{1,0:T(4,128)S(1)} all-reduce(f32[4,384]{1,0:T(4,128)S(1)} %bitcast.229), channel_id=1, replica_groups=mesh['ctx'=16,'head'=8] {'head'}, use_global_device_ids=true, to_apply=%region_13.14 | all-reduce | flops 1536 | bytes 12288 | tf_op jit(solution)/shard_map/psum | solution.py:159
  (340 shorter events, 453.7 us)
Async XLA Ops:
  6.5 66.6 %all-gather.7.cloned.1.call-start = ((), (), s32[]{:S(2)}) async-start(), calls=%async_computation.1 | async-start | bytes 3342336 | tf_op jit(solution)/shard_map/all_gather | solution.py:20
  14.6 4.4 copy-start.11
  18.0 4.2 copy-start.2
  19.0 4.0 copy-start.5
  22.3 174.2 %all-gather.5.cloned.1.call-start = ((), (), s32[]{:S(2)}) async-start(), calls=%async_computation | async-start | bytes 20054016 | tf_op jit(solution)/shard_map/all_gather | solution.py:101
  33.0 3.9 copy-start.10
  33.0 4.5 copy-start.3
  33.0 25.3 %copy-start.9 = (s32[4,3,16]{2,0,1:T(4,128)S(1)}, s32[4,3,16]{2,0,1:T(4,128)}, u32[]{:S(2)}) copy-start(s32[4,3,16]{2,0,1:T(4,128)} %param.11) | copy-start | bytes 2308
  36.9 55.3 %copy-start = (bf16[4,3,128,2,4,96]{2,5,4,3,1,0:T(8,128)(2,1)}, bf16[4,3,128,2,4,96]{2,5,4,3,1,0:T(8,128)(2,1)S(1)}, u32[]{:S(2)}) copy-start(bf16[4,3,128,2,4,96]{2,5,4,3,1,0:T(8,128)(2,1)S(1)} %fusion.42) | copy-start | bytes 7077892
  59.0 1.7 copy-start.6
  92.2 1.1 copy-start.8
  92.2 1.7 copy-start.4
  93.2 103.8 %copy-start.12 = (s32[4]{0:T(128)S(1)}, s32[4]{0:T(128)}, u32[]{:S(2)}) copy-start(s32[4]{0:T(128)} %param.12) | copy-start | bytes 52
  708.6 6.2 copy-start.1
  730.7 20.7 %copy-start.7 = (f32[768]{0:T(1024)S(1)}, f32[768]{0:T(1024)}, u32[]{:S(2)}) copy-start(f32[768]{0:T(1024)} %convert_element_type.87) | copy-start | bytes 9220
Sparse Core Ops, SparseCore 0:
  22.4 50.7 all-gather.6
  75.3 121.1 all-gather.4
where the time goes:
time: 771 us; the launch traced here: 764 us
  local copies, waits for them, and re-layouts  322 us (42%)
  matrix products  139 us (18%)
  other arithmetic  121 us (16%)
  waiting for transfers between devices  113 us (15%)
  blocking collectives  32.2 us (4%)
  loops' own time  23.4 us (3%)
  between operations  13.6 us (2%)
    gather x36, local copies, waits for them, and re-layouts, attend(): jnp.take(seq_pool, block_slots, axis=0).reshape(TOPK * BLK, kv_local, 2, HD)  180 us
    all_gather x1, waiting for transfers between devices, on_device(): candidates = lax.all_gather(kv_blocks, 'ctx', axis=1, tiled=True)  102 us
    sub x12, matrix products, attend(): weights = jnp.where(allowed[None, None], jnp.exp(scores - top_score), 0.0)  86.6 us
    squeeze x12, local copies, waits for them, and re-layouts, attend(): seq_pool = lax.dynamic_index_in_dim(candidates, seq_index, 0, False)  64 us
    dot_general x12, matrix products, attend(): jnp.einsum('ghxk,kge->xghe', weights.astype(jnp.bfloat16), picked[:, :, 1...  35.8 us
    select_n x24, other arithmetic, attend(): jnp.take(seq_pool, block_slots, axis=0).reshape(TOPK * BLK, kv_local, 2, HD)  26.6 us
    another operation x1, loops' own time, on_device(): lax.map(attend, jnp.arange(seq_count * stretch_count, dtype=jnp.int32))  22.9 us
    and x12, other arithmetic, attend(): listed[None, :] & (key_pos[None, :] <= query_pos[:, None])  20.8 us
  transfers between devices with their start and end apart: 2, of which 2 were waited for; matrix products, arithmetic and copies ran while one was open for 5% of the time, Pallas kernels for 0%

commit v1 on v0

v1 whole, which is shorter than its diff:
```python
import math

import jax
import jax.numpy as jnp
from jax import lax
from jax.experimental import pallas as pl
from jax.experimental.pallas import tpu as pltpu
from jax.sharding import PartitionSpec as P

HD = 96
BLK = 128
TOPK = 16
QBS = 3
NCTX = 16
GROUP = 4
LANES = 128
OWN = QBS
SLOTS = 20
epsilon = 1e-06
NEG = -1e30
SCALE = math.log2(math.e) / math.sqrt(HD)
NT = (((1,), (1,)), ((), ()))
TN = (((0,), (0,)), ((), ()))
NN = (((1,), (0,)), ((), ()))


def dot(a, b, dims):
    return lax.dot_general(a, b, dims, preferred_element_type=jnp.float32)


def feature(x):
    x = x.astype(jnp.float32)
    return jnp.where(x > 0, x + 1.0, jnp.exp(jnp.minimum(x, 0.0)))


def place(block, bias, kx, vx, slot):
    rows = pl.ds(pl.multiple_of(slot * BLK, BLK), BLK)
    ones = jnp.ones((BLK, LANES - HD), jnp.bfloat16)
    for g in range(2):
        k = block[:, 2 * g * HD : (2 * g + 1) * HD]
        v = block[:, (2 * g + 1) * HD : (2 * g + 2) * HD]
        kx[g, rows, :] = jnp.concatenate([k, bias], axis=1)
        vx[g, rows, :] = jnp.concatenate([v, ones], axis=1)


def kernel(
    starts, picks, q_ref, kv_ref, recv_ref, bias_ref, prior_ref, out_ref, kx, vx, qx, fq, fk, sc, mx
):
    b = pl.program_id(0)
    me = lax.axis_index("ctx")
    start = starts[b]
    tail = LANES - HD
    lane = lax.broadcasted_iota(jnp.int32, (BLK, tail), 1)
    row = lax.broadcasted_iota(jnp.int32, (BLK, tail), 0)
    wide_lane = lax.broadcasted_iota(jnp.int32, (BLK, LANES), 1)
    wide_row = lax.broadcasted_iota(jnp.int32, (BLK, LANES), 0)

    @pl.when(b == 0)
    def _():
        for g in range(2):
            kx[g] = jnp.full((SLOTS * BLK, LANES), NEG, jnp.bfloat16)
            kx[g, :, 0:HD] = jnp.zeros((SLOTS * BLK, HD), jnp.bfloat16)
            vx[g] = jnp.zeros((SLOTS * BLK, LANES), jnp.bfloat16)

    def tail_bias(slot_row, first_pos):
        listed = bias_ref[0, pl.ds(slot_row, 1), HD:LANES]
        late = jnp.where((lane == QBS) & (row + first_pos < start), NEG, 0.0)
        return (listed + late).astype(jnp.bfloat16)

    for k in range(QBS):
        pos = (me * QBS + k) * BLK
        block = kv_ref[0, k * BLK : (k + 1) * BLK, :]
        place(block, tail_bias(NCTX + k, pos), kx, vx, k)
        for g in range(2):
            f = feature(block[:, 2 * g * HD : (2 * g + 1) * HD])
            live = lax.broadcasted_iota(jnp.int32, (BLK, HD), 0) + pos >= start
            f = jnp.where(live, f, 0.0).astype(jnp.bfloat16)
            fk[g, k * BLK : (k + 1) * BLK, :] = jnp.concatenate(
                [f, jnp.zeros((BLK, tail), jnp.bfloat16)], axis=1
            )

    def bring(s, carry):
        pos = (s * QBS + picks[b, s]) * BLK
        place(recv_ref[0, s], tail_bias(s, pos), kx, vx, OWN + s)
        return carry

    lax.fori_loop(0, me, bring, 0)

    for qb in range(QBS):
        marks = jnp.where((lane == qb) | (lane == QBS), 1.0, 0.0).astype(jnp.bfloat16)
        for h in range(2 * GROUP):
            g, x = h // GROUP, h % GROUP
            piece = q_ref[0, qb * BLK : (qb + 1) * BLK, h * HD : (h + 1) * HD]
            base = (qb * 2 + g) * GROUP * BLK + x * BLK
            qx[base : base + BLK, :] = jnp.concatenate([piece, marks], axis=1)
            fq[base : base + BLK, :] = jnp.concatenate(
                [feature(piece).astype(jnp.bfloat16), jnp.zeros((BLK, tail), jnp.bfloat16)], axis=1
            )

    causal = wide_row >= wide_lane
    rows = GROUP * BLK
    causal4 = jnp.concatenate([causal] * GROUP, axis=0)
    chunks = (me + OWN + 1) // 2
    for g in range(2):
        state = prior_ref[0, g]
        for qb in range(QBS):
            base = (qb * 2 + g) * rows
            q = qx[base : base + rows, :]
            diag = dot(q, kx[g, qb * BLK : (qb + 1) * BLK, :], NT)
            diag = jnp.where(causal4, diag, NEG)
            sc[:, qb * BLK : (qb + 1) * BLK] = diag
            top = diag
            for k in range(QBS):
                if k < qb:
                    s = dot(q, kx[g, k * BLK : (k + 1) * BLK, :], NT)
                    top = jnp.maximum(top, s)
                    sc[:, k * BLK : (k + 1) * BLK] = s
                elif k > qb:
                    sc[:, k * BLK : (k + 1) * BLK] = jnp.full((rows, BLK), NEG, jnp.float32)
            s = dot(q, kx[g, OWN * BLK : (OWN + 1) * BLK, :], NT)
            sc[:, OWN * BLK : (OWN + 1) * BLK] = s
            mx[...] = jnp.maximum(top, s)

            def score(c, carry):
                at = pl.ds(pl.multiple_of(c * 2 * BLK, 2 * BLK), 2 * BLK)
                s = dot(q, kx[g, at, :], NT)
                sc[:, at] = s
                mx[...] = jnp.maximum(mx[...], jnp.maximum(s[:, :BLK], s[:, BLK:]))
                return carry

            lax.fori_loop(2, chunks, score, 0)
            peak = jnp.max(mx[...], axis=1, keepdims=True)

            def weigh(c, acc):
                at = pl.ds(pl.multiple_of(c * 2 * BLK, 2 * BLK), 2 * BLK)
                w = jnp.exp2((sc[:, at] - peak) * SCALE).astype(jnp.bfloat16)
                return acc + dot(w, vx[g, at, :], NN)

            acc = lax.fori_loop(0, chunks, weigh, jnp.zeros((rows, LANES), jnp.float32))
            fqv = fq[base : base + rows, :]
            fkv = fk[g, qb * BLK : (qb + 1) * BLK, :]
            vown = vx[g, qb * BLK : (qb + 1) * BLK, :]
            inner = jnp.where(causal4, dot(fqv, fkv, NT), 0.0).astype(jnp.bfloat16)
            high = state.astype(jnp.bfloat16)
            low = (state - high.astype(jnp.float32)).astype(jnp.bfloat16)
            lin = dot(inner, vown, NN) + dot(fqv, high, NN) + dot(fqv, low, NN)
            if qb < QBS - 1:
                state = state + dot(fkv, vown, TN)
            live = lax.broadcasted_iota(jnp.int32, (BLK, 1), 0) + (me * QBS + qb) * BLK >= start
            live4 = jnp.concatenate([live] * GROUP, axis=0)
            den = jnp.where(live4, lin[:, HD : HD + 1], 1.0)
            both = lin * (1.0 / den) + acc * (1.0 / acc[:, HD : HD + 1])
            both = jnp.where(live4, both, 0.0)
            out_ref[0, qb * BLK : (qb + 1) * BLK, g * GROUP * HD : (g + 1) * GROUP * HD] = (
                jnp.concatenate(
                    [both[x * BLK : (x + 1) * BLK, :HD] for x in range(GROUP)], axis=1
                )
            )


def on_device(queries, keys_values, block_lists, starts, norm_gain):
    nseq, length, width = queries.shape
    kv_width = keys_values.shape[2]
    me = lax.axis_index("ctx")
    ctx = jnp.arange(NCTX, dtype=jnp.int32)
    owner = jnp.where(block_lists >= 0, block_lists // QBS, -1)
    hit = owner[..., None] == ctx
    picks = jnp.max(jnp.where(hit, (block_lists % QBS)[..., None], 0), axis=(1, 2))
    listed = jnp.any(hit, axis=2)
    own = jnp.any(
        block_lists[..., None] == me * QBS + jnp.arange(QBS, dtype=jnp.int32), axis=2
    )
    flags = jnp.concatenate([listed, own, jnp.zeros_like(own)[..., :2]], axis=2)
    flags = jnp.where(flags, 0.0, NEG)
    bias = jnp.pad(
        jnp.transpose(flags, (0, 2, 1)), ((0, 0), (0, 0), (HD, LANES - HD - QBS))
    )
    wanted = lax.dynamic_index_in_dim(lax.all_gather(picks, "ctx", axis=0), me, 2, False)
    blocks = keys_values.reshape(nseq, QBS, BLK, kv_width)
    sent = jnp.stack(
        [
            jnp.where(
                (wanted[:, b] == 0)[:, None, None],
                blocks[b, 0],
                jnp.where((wanted[:, b] == 1)[:, None, None], blocks[b, 1], blocks[b, 2]),
            )
            for b in range(nseq)
        ]
    )
    recv = lax.all_to_all(sent, "ctx", 1, 1, tiled=True)

    positions = me * length + jnp.arange(length, dtype=jnp.int32)
    usable = positions[None, :] >= starts[:, None]
    pairs = keys_values.reshape(nseq, length, 2, 2, HD)
    phi = (feature(pairs[:, :, :, 0]) * usable[:, :, None, None]).astype(jnp.bfloat16)
    vals = jnp.concatenate(
        [pairs[:, :, :, 1], jnp.ones((nseq, length, 2, LANES - HD), jnp.bfloat16)], axis=3
    )
    state = jnp.einsum("btgd,btge->bgde", phi, vals, preferred_element_type=jnp.float32)
    every = lax.all_gather(state.astype(jnp.bfloat16), "ctx")
    prior = jnp.sum(
        jnp.where((ctx < me)[:, None, None, None, None], every.astype(jnp.float32), 0.0), axis=0
    )
    prior = jnp.pad(prior, ((0, 0), (0, 0), (0, LANES - HD), (0, 0)))

    smem = pl.BlockSpec(memory_space=pltpu.SMEM)
    combined = pl.pallas_call(
        kernel,
        grid=(nseq,),
        in_specs=[
            smem,
            smem,
            pl.BlockSpec((1, length, width), lambda b: (b, 0, 0)),
            pl.BlockSpec((1, length, kv_width), lambda b: (b, 0, 0)),
            pl.BlockSpec((1, NCTX, BLK, kv_width), lambda b: (b, 0, 0, 0)),
            pl.BlockSpec((1, NCTX + QBS + 2, LANES), lambda b: (b, 0, 0)),
            pl.BlockSpec((1, 2, LANES, LANES), lambda b: (b, 0, 0, 0)),
        ],
        out_specs=pl.BlockSpec((1, length, width), lambda b: (b, 0, 0)),
        out_shape=jax.ShapeDtypeStruct((nseq, length, width), jnp.float32),
        scratch_shapes=[
            pltpu.VMEM((2, SLOTS * BLK, LANES), jnp.bfloat16),
            pltpu.VMEM((2, SLOTS * BLK, LANES), jnp.bfloat16),
            pltpu.VMEM((QBS * 2 * GROUP * BLK, LANES), jnp.bfloat16),
            pltpu.VMEM((QBS * 2 * GROUP * BLK, LANES), jnp.bfloat16),
            pltpu.VMEM((2, QBS * BLK, LANES), jnp.bfloat16),
            pltpu.VMEM((GROUP * BLK, SLOTS * BLK), jnp.float32),
            pltpu.VMEM((GROUP * BLK, LANES), jnp.float32),
        ],
        compiler_params=pltpu.CompilerParams(vmem_limit_bytes=48 << 20),
    )(starts, picks, queries, keys_values, recv, bias, prior)

    squares = jnp.sum(combined * combined, axis=-1)
    all_squares = lax.psum(squares, "head")
    full_width = width * lax.axis_size("head")
    scaled = (
        combined
        * lax.rsqrt(all_squares / full_width + epsilon)[..., None]
        * norm_gain.astype(jnp.float32)
    )
    return scaled.astype(jnp.bfloat16)


def solution(mesh):
    return jax.shard_map(
        on_device,
        mesh=mesh,
        in_specs=(
            P(None, "ctx", "head"),
            P(None, "ctx", "head"),
            P(None, "ctx", None),
            P(),
            P("head"),
        ),
        out_specs=P(None, "ctx", "head"),
        check_vma=False,
    )
```

time: 771 us -> 298 us (0.39)
  the two profiles are of different devices: /device:TPU:1 before, /device:TPU:30 now
where the time goes in v1:
time: 298 us
  Pallas kernels  131 us (44%)
  waiting for transfers between devices  78.5 us (26%)
  blocking collectives  40.6 us (14%)
  other arithmetic  15.2 us (5%)
  between operations  13.6 us (5%)
  local copies, waits for them, and re-layouts  9.88 us (3%)
  starting transfers between devices  7.66 us (3%)
    pallas_call x1, Pallas kernels, on_device(): pl.pallas_call(kernel, grid=(nseq,), in_specs=[smem, smem, pl.BlockSpec((...  131 us
    all_gather x1, waiting for transfers between devices, on_device(): every = lax.all_gather(state.astype(jnp.bfloat16), 'ctx')  68.7 us
    all_gather x1, blocking collectives, on_device(): lax.all_gather(picks, 'ctx', axis=0)  21.1 us
    psum x1, blocking collectives, on_device(): all_squares = lax.psum(squares, 'head')  19.5 us
    all_to_all x1, waiting for transfers between devices, on_device(): recv = lax.all_to_all(sent, 'ctx', 1, 1, tiled=True)  9.78 us
    all_to_all x1, starting transfers between devices, on_device(): recv = lax.all_to_all(sent, 'ctx', 1, 1, tiled=True)  7.66 us
    all_to_all x1, local copies, waits for them, and re-layouts, on_device(): recv = lax.all_to_all(sent, 'ctx', 1, 1, tiled=True)  6.76 us
  transfers between devices with their start and end apart: 2, of which 2 were waited for; matrix products, arithmetic and copies ran while one was open for 3% of the time, Pallas kernels for 0%

profile of v1, /device:TPU:30, one launch (start us, length us, event | category | flops | bytes accessed | tf_op | source)
XLA Modules:
  0.0 298.0 jit_solution(3349875979279603003)
XLA Ops:
  6.5 1.7 copy.44
  8.3 0.4 copy.47
  8.7 0.2 copy-done.2
  9.0 1.3 convolution_convert_fusion
  10.3 0.1 select_reduce_fusion.picks
  10.5 21.1 %all-gather.2 = s32[16,4,16]{2,1,0:T(4,128)S(1)} all-gather(s32[1,4,16]{2,1,0:T(4,128)S(1)} %bitcast.56), channel_id=2, replica_groups=mesh['ctx'=16,'head'=8] {'ctx'}, dimensions={0}, use_global_device_ids=true | all-gather | bytes 4352 | tf_op jit(solution)/shard_map/all_gather | solution.py:178
  31.6 0.1 copy.40
  31.8 0.1 slice_bitcast_fusion.11
  31.9 0.6 select_select_fusion.2
  32.6 0.6 select_select_fusion
  33.2 3.5 %pad_maximum_fusion = bf16[4,16,128,384]{3,2,0,1:T(8,128)(2,1)} fusion(bf16[1,16,128,384]{3,2,0,1:T(8,128)(2,1)S(1)} %get-tuple-element.27, bf16[1,16,128,384]{3,2,0,1:T(8,128)(2,1)S(1)} %get-tuple-element.28, bf16[1,16,128,384]{3,2,0,1:T(8,128)(2,1)S(1)} %get-tuple-element.29, bf16[1,16,128,384]{3,2,0,1:T(8,128)(2,1)S(1)} %get-tuple-element.30), kind=kLoop, calls=%fused_computation | loop fusion | flops 9437184 | bytes 12582912 | tf_op jit(solution)/shard_map/stack | solution.py:180
  36.8 7.7 %all-to-all-start = ((bf16[4,16,128,384]{3,2,0,1:T(8,128)(2,1)}), bf16[4,16,128,384]{3,2,0,1:T(8,128)(2,1)}, u32[]{:S(2)}, u32[]{:S(2)}) async-start(bf16[4,16,128,384]{3,2,0,1:T(8,128)(2,1)} %pad_maximum_fusion), calls=%async_computation | async-start | bytes 12582912 | tf_op jit(solution)/shard_map/all_to_all | solution.py:190
  44.4 0.3 compare_reduce_fusion
  44.7 0.1 copy.42
  44.9 0.1 fusion.12
  45.2 0.1 copy.43
  45.4 68.7 %all-gather.5.cloned.1.call-done = bf16[64,2,96,128]{3,2,1,0:T(8,128)(2,1)} async-done(((bf16[4,2,96,128]{3,2,1,0:T(8,128)(2,1)}), bf16[64,2,96,128]{3,2,1,0:T(8,128)(2,1)}) %all-gather.5.cloned.1.call-update) | async-done | bytes 3145744 | tf_op jit(solution)/shard_map/all_gather | solution.py:200
  114.1 2.6 fusion
  116.8 9.8 %all-to-all-done = bf16[4,16,128,384]{3,2,0,1:T(8,128)(2,1)} async-done(((bf16[4,16,128,384]{3,2,0,1:T(8,128)(2,1)}), bf16[4,16,128,384]{3,2,0,1:T(8,128)(2,1)}, u32[]{:S(2)}, u32[]{:S(2)}) %all-to-all-start) | async-done | bytes 6291488 | tf_op jit(solution)/shard_map/all_to_all | solution.py:190
  126.6 6.8 %copy.46.recv_ref = bf16[4,16,128,384]{3,2,1,0:T(8,128)(2,1)} copy(bf16[4,16,128,384]{3,2,0,1:T(8,128)(2,1)} %all-to-all-done) | data formatting | bytes 12582912 | tf_op jit(solution)/shard_map/all_to_all | solution.py:190
  133.3 131.3 %shard_map.55 = f32[4,384,768]{2,1,0:T(8,128)} custom-call(s32[4]{0:T(128)S(1)} %copy-done.2, s32[4,16]{1,0:T(4,128)S(1)} %select_reduce_fusion.picks, bf16[4,384,768]{2,1,0:T(8,128)(2,1)S(1)} %copy-done.1, bf16[4,384,384]{2,1,0:T(8,128)(2,1)S(1)} %copy-done, bf16[4,16,128,384]{3,2,1,0:T(8,128)(2,1)} %copy.46.recv_ref, f32[4,21,128]{2,1,0:T(8,128)S(1)} %pad.9.bias_ref, ...), custom_call_target="tpu_custom_call" | custom-call | tf_op jit(solution)/shard_map/pallas_call | solution.py:207
  264.6 2.7 multiply_reduce_fusion
  267.4 19.5 %psum.7 = f32[4,384]{1,0:T(4,128)S(1)} all-reduce(f32[4,384]{1,0:T(4,128)S(1)} %multiply_reduce_fusion), channel_id=1, replica_groups=mesh['ctx'=16,'head'=8] {'head'}, use_global_device_ids=true, to_apply=%region_5.6 | all-reduce | flops 1536 | bytes 12288 | tf_op jit(solution)/shard_map/psum | solution.py:234
  286.9 4.2 %multiply_convert_fusion = bf16[4,384,768]{2,1,0:T(8,128)(2,1)} fusion(f32[4,384,768]{2,1,0:T(8,128)} %shard_map.55, f32[768]{0:T(1024)S(1)} %convert_element_type.36, f32[4,384]{1,0:T(4,128)S(1)} %add_rsqrt_fusion), kind=kLoop, calls=%fused_computation.3 | loop fusion | flops 3538944 | bytes 7087104 | tf_op jit(solution)/shard_map/convert_element_type | solution.py:241
  (29 shorter events, 0.6 us)
Async XLA Ops:
  6.5 107.6 %all-gather.5.cloned.1.call-start = ((), (), s32[]{:S(2)}) async-start(), calls=%async_computation.1 | async-start | bytes 3342336 | tf_op jit(solution)/shard_map/all_gather | solution.py:200
  8.3 0.7 copy-start.2
  9.0 1.3 copy-start.3
  9.0 22.8 %copy-start = (bf16[4,384,384]{2,1,0:T(8,128)(2,1)S(1)}, bf16[4,384,384]{2,1,0:T(8,128)(2,1)}, u32[]{:S(2)}) copy-start(bf16[4,384,384]{2,1,0:T(8,128)(2,1)} %kv_ref.1) | copy-start | bytes 3538948
  36.7 8.5 %copy-start.4 = (bf16[768]{0:T(1024)(128)(2,1)S(1)}, bf16[768]{0:T(1024)(128)(2,1)}, u32[]{:S(2)}) copy-start(bf16[768]{0:T(1024)(128)(2,1)} %param.9) | copy-start | bytes 4612
  36.8 89.8 %all-to-all-start = ((bf16[4,16,128,384]{3,2,0,1:T(8,128)(2,1)}), bf16[4,16,128,384]{3,2,0,1:T(8,128)(2,1)}, u32[]{:S(2)}, u32[]{:S(2)}) async-start(bf16[4,16,128,384]{3,2,0,1:T(8,128)(2,1)} %pad_maximum_fusion), calls=%async_computation | async-start | bytes 12582912 | tf_op jit(solution)/shard_map/all_to_all | solution.py:190
  126.6 6.8 %copy-start.1 = (bf16[4,384,768]{2,1,0:T(8,128)(2,1)S(1)}, bf16[4,384,768]{2,1,0:T(8,128)(2,1)}, u32[]{:S(2)}) copy-start(bf16[4,384,768]{2,1,0:T(8,128)(2,1)} %q_ref.1) | copy-start | bytes 7077892
Sparse Core Ops, SparseCore 0:
  10.4 103.6 all-gather.4

commit v2 on v0

v2 whole, which is shorter than its diff:
```python
import math

import jax
import jax.numpy as jnp
from jax import lax
from jax.experimental import pallas as pl
from jax.experimental.pallas import tpu as pltpu
from jax.sharding import PartitionSpec as P

HD = 96
BLK = 128
QBS = 3
NSEQ = 4
SIDE = 4
NCTX = 16
NHEAD = 8
GROUP = 4
LANES = 128
LEN = QBS * BLK
KVW = 4 * HD
WIDTH = 2 * GROUP * HD
ROWS = GROUP * BLK
OWN0 = NCTX - 1
SLOTS = OWN0 + QBS
NCH = SLOTS // 2
TAIL = LANES - HD
epsilon = 1e-06
NEG = -1e30
SCALE = math.log2(math.e) / math.sqrt(HD)
NT = (((1,), (1,)), ((), ()))
TN = (((0,), (0,)), ((), ()))
NN = (((1,), (0,)), ((), ()))
BF = jnp.bfloat16
F32 = jnp.float32
MESH = pl.DeviceIdType.MESH


def dot(a, b, dims):
    return lax.dot_general(a, b, dims, preferred_element_type=F32)


def feature(x):
    x = x.astype(F32)
    return jnp.where(x > 0, x + 1.0, jnp.exp(jnp.minimum(x, 0.0)))


def kernel(
    starts, picks, q_hbm, kv, bias_ref, pickrows, gain, out_ref,
    q_ref, near, packed, far, relay, pk_in, st_own, st_y, st_row, st_x,
    prior, fk, vown, lin_ref, comb, kx, vx, qx, fq, sc, pw, mx, sq, sq_in,
    q_sem, s_send, s_recv, p_send, p_recv, t_send, t_recv, h_send, h_recv,
):
    me = lax.axis_index("ctx")
    hd = lax.axis_index("head")
    x, y = me // SIDE, me % SIDE

    def device(o, du, dv):
        dx, dy = (du, dv) if o == 0 else (dv, du)
        return ((x + dx + 2 * SIDE) % SIDE) * SIDE + (y + dy + 2 * SIDE) % SIDE

    def copy(src, dst, send, recv, target):
        return pltpu.make_async_remote_copy(
            src_ref=src, dst_ref=dst, send_sem=send, recv_sem=recv,
            device_id={"ctx": target}, device_id_type=MESH,
        )

    q_copy = pltpu.make_async_copy(q_hbm, q_ref, q_sem)
    q_copy.start()
    barrier = pltpu.get_barrier_semaphore()
    for o in range(2):
        for d in range(1, SIDE):
            pl.semaphore_signal(
                barrier, inc=1, device_id={"ctx": device(o, d, 0)}, device_id_type=MESH
            )
    for d in range(1, NHEAD):
        pl.semaphore_signal(
            barrier, inc=1, device_id={"head": (hd + d) % NHEAD}, device_id_type=MESH
        )
    pl.semaphore_wait(barrier, 2 * (SIDE - 1) + NHEAD - 1)

    def pick_copy(o, d):
        i = o * 3 + d - 1
        return copy(pickrows, pk_in.at[o, d - 1], p_send.at[i], p_recv.at[i], device(o, 0, -d))

    def hop(b, i):
        o = b % 2
        half = LEN // 2
        src, dst, du, dv = [
            (kv.at[b], near.at[b, 0], 1, 0),
            (kv.at[b], near.at[b, 2], -1, 0),
            (near.at[b, 0, 0:half], near.at[b, 1, 0:half], 1, 0),
            (near.at[b, 2, half:LEN], near.at[b, 1, half:LEN], -1, 0),
            (packed.at[b, 0], far.at[b, 0], 0, 1),
            (packed.at[b, 2], far.at[b, 2], 0, -1),
            (packed.at[b, 1, 0:2], relay.at[b, 0], 0, 1),
            (packed.at[b, 1, 2:4], relay.at[b, 1], 0, -1),
            (relay.at[b, 0], far.at[b, 1, 0:2], 0, 1),
            (relay.at[b, 1], far.at[b, 1, 2:4], 0, -1),
        ][i]
        return copy(src, dst, s_send.at[b, i], s_recv.at[b, i], device(o, du, dv))

    def start(b, *which):
        for i in which:
            hop(b, i).start()

    def arrived(b, *which):
        for i in which:
            hop(b, i).wait_recv()

    for b in (0, 1):
        start(b, 0, 1)
    for o in range(2):
        for d in range(1, SIDE):
            pick_copy(o, d).start()

    row96 = lax.broadcasted_iota(jnp.int32, (BLK, HD), 0)
    lane = lax.broadcasted_iota(jnp.int32, (BLK, TAIL), 1)
    row = lax.broadcasted_iota(jnp.int32, (BLK, TAIL), 0)
    zeros = jnp.zeros((BLK, TAIL), BF)
    ones = jnp.ones((BLK, TAIL), BF)

    def summary(b, carry):
        first = starts[b]
        for k in range(QBS):
            at = slice(k * BLK, (k + 1) * BLK)
            live = row96 + (me * QBS + k) * BLK >= first
            for g in range(2):
                key = kv[b, at, 2 * g * HD : (2 * g + 1) * HD]
                f = jnp.where(live, feature(key), 0.0).astype(BF)
                fk[b, g, at, :] = jnp.concatenate([f, zeros], axis=1)
                v = kv[b, at, (2 * g + 1) * HD : (2 * g + 2) * HD]
                vown[b, g, at, :] = jnp.concatenate([v, ones], axis=1)
        for g in range(2):
            t = dot(fk[b, g], vown[b, g], TN)
            st_own[b, g] = t[:HD].astype(BF)
        return carry

    lax.fori_loop(0, NSEQ, summary, 0)

    def state_copy(o, d):
        i = (1 - o) * 3 + d - 1
        src, dst = (st_row, st_x) if o == 0 else (st_own, st_y)
        return copy(src, dst.at[d - 1], t_send.at[i], t_recv.at[i], device(o, d, 0))

    for d in range(1, SIDE):
        state_copy(1, d).start()
    for b in (0, 1):
        arrived(b, 0, 1)
        start(b, 2, 3)
    for d in range(1, SIDE):
        state_copy(1, d).wait_recv()

    def rows_sum(b, carry):
        for g in range(2):
            total = st_own[b, g].astype(F32)
            before = jnp.zeros((HD, LANES), F32)
            for d in range(1, SIDE):
                part = st_y[d - 1, b, g].astype(F32)
                total = total + part
                before = before + jnp.where(y >= d, part, 0.0)
            st_row[b, g] = total.astype(BF)
            prior[b, g] = before
        return carry

    lax.fori_loop(0, NSEQ, rows_sum, 0)
    for d in range(1, SIDE):
        state_copy(0, d).start()
    for o in range(2):
        for d in range(1, SIDE):
            pick_copy(o, d).wait_recv()

    def source(o, du, dv):
        return device(o, -du, -dv)

    def choose(table, at, blocks, put):
        w = jnp.broadcast_to(table[pl.ds(at, 1), :], (BLK, LANES)).astype(BF)
        m0, m1 = w == 0.0, w == 1.0
        for c in range(KVW // LANES):
            cols = slice(c * LANES, (c + 1) * LANES)
            b0, b1, b2 = [blocks[k * BLK : (k + 1) * BLK, cols] for k in range(QBS)]
            put(cols, jnp.where(m0, b0, jnp.where(m1, b1, b2)))

    def pack(b):
        o = b % 2
        for dv in range(1, SIDE):
            for du in range(SIDE):
                blocks = kv.at[b] if du == 0 else near.at[b, du - 1]

                def put(cols, val, dv=dv, du=du):
                    packed[b, dv - 1, du, :, cols] = val

                choose(pk_in.at[o, dv - 1], b * NCTX + source(o, du, 0), blocks, put)

    for b in (0, 1):
        arrived(b, 2, 3)
        pack(b)
        start(b, 4, 5, 6, 7)
    for b in (2, 3):
        start(b, 0, 1)

    for d in range(1, SIDE):
        state_copy(0, d).wait_recv()

    def add_x(b, carry):
        for g in range(2):
            before = prior[b, g]
            for d in range(1, SIDE):
                before = before + jnp.where(x >= d, st_x[d - 1, b, g].astype(F32), 0.0)
            prior[b, g] = before
        return carry

    lax.fori_loop(0, NSEQ, add_x, 0)
    q_copy.wait()

    trow = lax.broadcasted_iota(jnp.int32, (ROWS, BLK), 0) % BLK
    tlane = lax.broadcasted_iota(jnp.int32, (ROWS, BLK), 1)
    causal = trow >= tlane

    def live_rows(b, qb):
        r = lax.broadcasted_iota(jnp.int32, (ROWS, 1), 0) % BLK
        return r + (me * QBS + qb) * BLK >= starts[b]

    def linear(b, carry):
        for g in range(2):
            state = jnp.concatenate([prior[b, g], jnp.zeros((TAIL, LANES), F32)], axis=0)
            for qb in range(QBS):
                for h in range(GROUP):
                    c = (g * GROUP + h) * HD
                    piece = q_ref[b, qb * BLK : (qb + 1) * BLK, c : c + HD]
                    fq[qb % 2, h * BLK : (h + 1) * BLK, :] = jnp.concatenate(
                        [feature(piece).astype(BF), zeros], axis=1
                    )
                fqv = fq[qb % 2]
                fkv = fk[b, g, qb * BLK : (qb + 1) * BLK, :]
                vo = vown[b, g, qb * BLK : (qb + 1) * BLK, :]
                inner = jnp.where(causal, dot(fqv, fkv, NT), 0.0).astype(BF)
                high = state.astype(BF)
                low = (state - high.astype(F32)).astype(BF)
                lin = dot(inner, vo, NN) + dot(fqv, high, NN) + dot(fqv, low, NN)
                if qb < QBS - 1:
                    state = state + dot(fkv, vo, TN)
                den = jnp.where(live_rows(b, qb), lin[:, HD : HD + 1], 1.0)
                lin_ref[b, g * QBS + qb] = lin * (1.0 / den)
        return carry

    lax.fori_loop(0, 2, linear, 0)
    for b in (0, 1):
        arrived(b, 6, 7)
        start(b, 8, 9)
    for b in (2, 3):
        arrived(b, 0, 1)
        start(b, 2, 3)
    lax.fori_loop(2, NSEQ, linear, 0)
    for b in (2, 3):
        arrived(b, 2, 3)
        pack(b)
        start(b, 4, 5, 6, 7)

    def place(slot, load, bias):
        at = slice(slot * BLK, (slot + 1) * BLK)
        for g in range(2):
            k = load(2 * g * HD, (2 * g + 1) * HD)
            v = load((2 * g + 1) * HD, (2 * g + 2) * HD)
            kx[g, at, :] = jnp.concatenate([k, bias], axis=1)
            vx[g, at, :] = jnp.concatenate([v, ones], axis=1)

    def tail_bias(b, slot_row, pos):
        listed = bias_ref[b, pl.ds(slot_row, 1), HD:LANES]
        late = jnp.where((lane == QBS) & (row + pos < starts[b]), NEG, 0.0)
        return (listed + late).astype(BF)

    def scores(i):
        g, qb = i // QBS, i % QBS
        q = qx[i * ROWS : (i + 1) * ROWS, :]
        top = None
        for c in range(NCH):
            at = slice(c * 2 * BLK, (c + 1) * 2 * BLK)
            s = dot(q, kx[g, at, :], NT)
            parts = []
            for n in range(2):
                k = 2 * c + n - OWN0
                part = s[:, n * BLK : (n + 1) * BLK]
                if k == qb:
                    part = jnp.where(causal, part, NEG)
                parts.append(part)
                sc[i % 2, :, (2 * c + n) * BLK : (2 * c + n + 1) * BLK] = part
            t = jnp.maximum(parts[0], parts[1])
            top = t if top is None else jnp.maximum(top, t)
        mx[i % 2] = top

    def weigh(b, i):
        g, qb = i // QBS, i % QBS
        peak = jnp.max(mx[i % 2], axis=1, keepdims=True)
        for c in range(NCH):
            at = slice(c * 2 * BLK, (c + 1) * 2 * BLK)
            pw[i % 2, :, at] = jnp.exp2((sc[i % 2, :, at] - peak) * SCALE).astype(BF)
        acc = dot(pw[i % 2], vx[g], NN)
        both = lin_ref[b, i] + acc * (1.0 / acc[:, HD : HD + 1])
        both = jnp.where(live_rows(b, qb), both, 0.0)
        comb[b, qb * BLK : (qb + 1) * BLK, g * GROUP * HD : (g + 1) * GROUP * HD] = (
            jnp.concatenate([both[h * BLK : (h + 1) * BLK, :HD] for h in range(GROUP)], axis=1)
        )

    def attend(b, carry):
        o = b % 2
        u_x = 1 - o

        for which in range(2):

            @pl.when(b == 2)
            def _(which=which):
                arrived(2 + which, 6, 7)
                start(2 + which, 8, 9)

        for which in range(NSEQ):

            @pl.when(b == which)
            def _(which=which):
                arrived(which, 4, 5, 8, 9)

        def source_of(du, dv):
            sx = (x + 8 - du * u_x - dv * o) % SIDE
            sy = (y + 8 - dv * u_x - du * o) % SIDE
            return sx * SIDE + sy

        slot = 0
        for dv in range(SIDE):
            for du in range(SIDE):
                if du == 0 and dv == 0:
                    continue
                s = source_of(du, dv)
                pos = (s * QBS + picks[b, s]) * BLK
                tb = tail_bias(b, s, pos)
                if dv == 0:
                    got = []
                    choose(
                        pickrows, b * NCTX + s, near.at[b, du - 1],
                        lambda cols, val, got=got: got.append(val),
                    )
                    whole = jnp.concatenate(got, axis=1)
                    place(slot, lambda l, r, w=whole: w[:, l:r], tb)
                else:
                    place(slot, lambda l, r, dv=dv, du=du: far[b, dv - 1, du, :, l:r], tb)
                slot += 1
        for k in range(QBS):
            tb = tail_bias(b, NCTX + k, (me * QBS + k) * BLK)
            place(slot, lambda l, r, k=k: kv[b, k * BLK : (k + 1) * BLK, l:r], tb)
            slot += 1
        for qb in range(QBS):
            marks = jnp.where((lane == qb) | (lane == QBS), 1.0, 0.0).astype(BF)
            for h in range(2 * GROUP):
                g, r = h // GROUP, h % GROUP
                piece = q_ref[b, qb * BLK : (qb + 1) * BLK, h * HD : (h + 1) * HD]
                base = (g * QBS + qb) * ROWS + r * BLK
                qx[base : base + BLK, :] = jnp.concatenate([piece, marks], axis=1)
        scores(0)
        for i in range(2 * QBS):
            if i + 1 < 2 * QBS:
                scores(i + 1)
            weigh(b, i)
        for qb in range(QBS):
            c = comb[b, qb * BLK : (qb + 1) * BLK, :]
            c2 = c * c
            high = c2.astype(BF)
            low = (c2 - high.astype(F32)).astype(BF)
            e = jnp.ones((8, WIDTH), BF)
            total = dot(e, high, NT) + dot(e, low, NT)
            sq[b * QBS + qb] = total
        return carry

    lax.fori_loop(0, NSEQ, attend, 0)

    def sq_copy(d):
        return pltpu.make_async_remote_copy(
            src_ref=sq, dst_ref=sq_in.at[d - 1], send_sem=h_send.at[d - 1],
            recv_sem=h_recv.at[d - 1], device_id={"head": (hd + d) % NHEAD}, device_id_type=MESH,
        )

    for d in range(1, NHEAD):
        sq_copy(d).start()
    for d in range(1, NHEAD):
        sq_copy(d).wait_recv()

    eye = lax.broadcasted_iota(jnp.int32, (BLK, BLK), 0) == lax.broadcasted_iota(
        jnp.int32, (BLK, BLK), 1
    )
    scale_by = gain[...].astype(F32)

    def finish(n, carry):
        total = sq[n, 0:1, :]
        for d in range(1, NHEAD):
            total = total + sq_in[d - 1, n, 0:1, :]
        r = lax.rsqrt(total / (WIDTH * NHEAD) + epsilon)
        col = jnp.sum(jnp.where(eye, jnp.broadcast_to(r, (BLK, BLK)), 0.0), axis=1, keepdims=True)
        b, qb = n // QBS, n % QBS
        at = pl.ds(pl.multiple_of(qb * BLK, BLK), BLK)
        out_ref[b, at, :] = (comb[b, at, :] * col * scale_by).astype(BF)
        return carry

    lax.fori_loop(0, NSEQ * QBS, finish, 0)

    for d in range(1, NHEAD):
        sq_copy(d).wait_send()
    for o in range(2):
        for d in range(1, SIDE):
            pick_copy(o, d).wait_send()
            state_copy(o, d).wait_send()
    for b in range(NSEQ):
        for i in range(10):
            hop(b, i).wait_send()


def on_device(queries, keys_values, block_lists, starts, norm_gain):
    me = lax.axis_index("ctx")
    ctx = jnp.arange(NCTX, dtype=jnp.int32)
    owner = jnp.where(block_lists >= 0, block_lists // QBS, -1)
    hit = owner[..., None] == ctx
    picks = jnp.max(jnp.where(hit, (block_lists % QBS)[..., None], 0), axis=(1, 2))
    listed = jnp.any(hit, axis=2)
    own = jnp.any(
        block_lists[..., None] == me * QBS + jnp.arange(QBS, dtype=jnp.int32), axis=2
    )
    flags = jnp.concatenate([listed, own, jnp.zeros_like(own)], axis=2)
    flags = jnp.concatenate([flags, jnp.zeros_like(own)[..., :2]], axis=2)
    flags = jnp.where(flags, 0.0, NEG)
    bias = jnp.pad(
        jnp.transpose(flags, (0, 2, 1)), ((0, 0), (0, 0), (HD, LANES - HD - QBS))
    )
    pickrows = jnp.broadcast_to(
        picks.reshape(NSEQ * NCTX, 1).astype(F32), (NSEQ * NCTX, LANES)
    )
    smem = pl.BlockSpec(memory_space=pltpu.SMEM)
    vmem = pl.BlockSpec(memory_space=pltpu.VMEM)
    dma = pltpu.SemaphoreType.DMA
    return pl.pallas_call(
        kernel,
        in_specs=[smem, smem, pl.BlockSpec(memory_space=pl.ANY), vmem, vmem, vmem, vmem],
        out_specs=vmem,
        out_shape=jax.ShapeDtypeStruct((NSEQ, LEN, WIDTH), BF),
        scratch_shapes=[
            pltpu.VMEM((NSEQ, LEN, WIDTH), BF),
            pltpu.VMEM((NSEQ, 3, LEN, KVW), BF),
            pltpu.VMEM((NSEQ, 3, SIDE, BLK, KVW), BF),
            pltpu.VMEM((NSEQ, 3, SIDE, BLK, KVW), BF),
            pltpu.VMEM((NSEQ, 2, 2, BLK, KVW), BF),
            pltpu.VMEM((2, 3, NSEQ * NCTX, LANES), F32),
            pltpu.VMEM((NSEQ, 2, HD, LANES), BF),
            pltpu.VMEM((3, NSEQ, 2, HD, LANES), BF),
            pltpu.VMEM((NSEQ, 2, HD, LANES), BF),
            pltpu.VMEM((3, NSEQ, 2, HD, LANES), BF),
            pltpu.VMEM((NSEQ, 2, HD, LANES), F32),
            pltpu.VMEM((NSEQ, 2, LEN, LANES), BF),
            pltpu.VMEM((NSEQ, 2, LEN, LANES), BF),
            pltpu.VMEM((NSEQ, 2 * QBS, ROWS, LANES), F32),
            pltpu.VMEM((NSEQ, LEN, WIDTH), F32),
            pltpu.VMEM((2, SLOTS * BLK, LANES), BF),
            pltpu.VMEM((2, SLOTS * BLK, LANES), BF),
            pltpu.VMEM((2 * QBS * ROWS, LANES), BF),
            pltpu.VMEM((2, ROWS, LANES), BF),
            pltpu.VMEM((2, ROWS, SLOTS * BLK), F32),
            pltpu.VMEM((2, ROWS, SLOTS * BLK), BF),
            pltpu.VMEM((2, ROWS, LANES), F32),
            pltpu.VMEM((NSEQ * QBS, 8, LANES), F32),
            pltpu.VMEM((NHEAD - 1, NSEQ * QBS, 8, LANES), F32),
            dma,
            dma((NSEQ, 10)),
            dma((NSEQ, 10)),
            dma((6,)),
            dma((6,)),
            dma((6,)),
            dma((6,)),
            dma((NHEAD - 1,)),
            dma((NHEAD - 1,)),
        ],
        compiler_params=pltpu.CompilerParams(
            vmem_limit_bytes=60 << 20, collective_id=0, has_side_effects=True
        ),
    )(starts, picks, queries, keys_values, bias, pickrows, norm_gain.reshape(1, WIDTH))


def solution(mesh):
    return jax.shard_map(
        on_device,
        mesh=mesh,
        in_specs=(
            P(None, "ctx", "head"),
            P(None, "ctx", "head"),
            P(None, "ctx", None),
            P(),
            P("head"),
        ),
        out_specs=P(None, "ctx", "head"),
        check_vma=False,
    )
```

time: 771 us -> 124 us (0.16)
  local copies, waits for them, and re-layouts: 322 us -> 6.38 us
  matrix products: 139 us -> 0 us
  other arithmetic: 121 us -> 2.05 us
  Pallas kernels: 0 us -> 115 us
  waiting for transfers between devices: 113 us -> 0 us
  blocking collectives: 32.2 us -> 0 us
  loops' own time: 23.4 us -> 0 us
  between operations: 13.6 us -> 0.06 us
    gather x36 -> x0, local copies, waits for them, and re-layouts: 180 us -> none  [attend(): jnp.take(seq_pool, block_slots, axis=0).reshape(TOPK * BLK, kv_local, 2, HD)]
    pallas_call x0 -> x1, Pallas kernels: none -> 115 us  [on_device(): pl.pallas_call(kernel, in_specs=[smem, smem, pl.BlockSpec(memory_space=pl...]
    all_gather x2 -> x0, waiting for transfers between devices: 112 us -> none  [the longest x1 102 us: on_device(): candidates = lax.all_gather(kv_blocks, 'ctx', axis=1, tiled=True)]
    sub x12 -> x0, matrix products: 86.6 us -> none  [attend(): weights = jnp.where(allowed[None, None], jnp.exp(scores - top_score), 0.0)]
    squeeze x12 -> x0, local copies, waits for them, and re-layouts: 64 us -> none  [attend(): seq_pool = lax.dynamic_index_in_dim(candidates, seq_index, 0, False)]
    dot_general x17 -> x0, matrix products: 52.7 us -> none  [the longest x12 35.8 us: attend(): jnp.einsum('ghxk,kge->xghe', weights.astype(jnp.bfloat16), picked[:, :, 1...]
    select_n x69 -> x2, other arithmetic: 45.9 us -> 0.79 us  [the longest x1 0.71 us: on_device(): owner = jnp.where(block_lists >= 0, block_lists // QBS, -1)]
    and x24 -> x0, other arithmetic: 28.7 us -> none  [the longest x12 20.8 us: attend(): listed[None, :] & (key_pos[None, :] <= query_pos[:, None])]
  transfers between devices with their start and end apart: 2 -> 0, of which waited for: 2 -> 0; matrix products, arithmetic and copies ran while one was open for 5% -> 0% of each run, Pallas kernels for 0% -> 0%
where the time goes in v2:
time: 124 us
  Pallas kernels  115 us (93%)
  local copies, waits for them, and re-layouts  6.38 us (5%)
  other arithmetic  2.05 us (2%)
    pallas_call x1, Pallas kernels, on_device(): pl.pallas_call(kernel, in_specs=[smem, smem, pl.BlockSpec(memory_space=pl...  115 us
    unnamed x3, local copies, waits for them, and re-layouts  3.23 us

profile of v2, /device:TPU:1, one launch (start us, length us, event | category | flops | bytes accessed | tf_op | source)
XLA Modules:
  0.0 123.8 jit_solution(15666900430504826561)
XLA Ops:
  0.0 0.1 pad.8.clone
  0.1 0.1 pad.7.clone
  0.2 1.0 compare_reduce_fusion
  1.2 0.1 copy.25
  1.3 1.3 %reshape.19.gain = bf16[1,768]{1,0:T(2,128)(2,1)} reshape(bf16[768]{0:T(1024)(128)(2,1)} %param.9) | data formatting | bytes 3072 | tf_op jit(solution)/shard_map/reshape | solution.py:478
  2.6 0.7 fusion.1
  3.3 0.1 fusion
  3.4 0.1 add_select_fusion.2
  3.5 0.1 select_reduce_fusion.picks
  3.7 0.0 copy-start
  3.7 0.1 convert_element_type.14
  3.8 0.7 broadcast_in_dim.40.pickrows
  4.4 0.1 copy.26
  4.5 0.7 pad.4.bias_ref
  5.2 0.0 copy-done
  5.3 115.3 %shard_map.55 = bf16[4,384,768]{2,1,0:T(8,128)(2,1)} custom-call(s32[4]{0:T(128)} %starts.1, s32[4,16]{1,0:T(4,128)} %copy-done, bf16[4,384,768]{2,1,0:T(8,128)(2,1)} %q_hbm.1, bf16[4,384,384]{2,1,0:T(8,128)(2,1)} %kv.1, f32[4,24,128]{2,1,0:T(8,128)} %pad.4.bias_ref, f32[64,128]{1,0:T(8,128)} %broadcast_in_dim.40.pickrows, bf16[1,768]{1,0:T(2,128)(2,1)} %reshape.19.gain), custom_call_target="tpu_custom_call" | custom-call | tf_op jit(solution)/shard_map/pallas_call | solution.py:435
  120.5 3.2 %copy.28 = bf16[4,384,768]{2,1,0:T(8,128)(2,1)} copy(bf16[4,384,768]{2,1,0:T(8,128)(2,1)} %shard_map.55) | data formatting | bytes 4718592
  (7 shorter events, 0.0 us)
Async XLA Ops:
  3.7 1.6 %copy-start = (s32[4,16]{1,0:T(4,128)}, s32[4,16]{1,0:T(4,128)S(1)}, u32[]{:S(2)}) copy-start(s32[4,16]{1,0:T(4,128)S(1)} %select_reduce_fusion.picks) | copy-start | bytes 772

commit v3 on v2

v3 whole, which is shorter than its diff:
```python
import math

import jax
import jax.numpy as jnp
from jax import lax
from jax.experimental import pallas as pl
from jax.experimental.pallas import tpu as pltpu
from jax.sharding import PartitionSpec as P

HD = 96
BLK = 128
QBS = 3
TOPK = 16
NSEQ = 4
SIDE = 4
NCTX = 16
NHEAD = 8
GROUP = 4
LANES = 128
LEN = QBS * BLK
KVW = 4 * HD
WIDTH = 2 * GROUP * HD
ROWS = GROUP * BLK
HALF = BLK // 2
OWN0 = NCTX - 1
SLOTS = OWN0 + QBS
NCH = SLOTS // 2
TAIL = LANES - HD
epsilon = 1e-06
NEG = -1e30
SCALE = math.log2(math.e) / math.sqrt(HD)
NT = (((1,), (1,)), ((), ()))
TN = (((0,), (0,)), ((), ()))
NN = (((1,), (0,)), ((), ()))
BF = jnp.bfloat16
F32 = jnp.float32
MESH = pl.DeviceIdType.MESH


def dot(a, b, dims):
    return lax.dot_general(a, b, dims, preferred_element_type=F32)


def feature(x):
    x = x.astype(F32)
    return jnp.where(x > 0, x + 1.0, jnp.exp(jnp.minimum(x, 0.0)))


def kernel(
    starts, lists, q_hbm, kv, gain, out_ref,
    q_ref, near, packed, far, relay, bias_ref, pickrows, pk_in, st_own, st_y, st_row, st_x,
    prior, fk, vown, lin_ref, comb, kx, vx, qx, fq, sc, pw, mx, sq, sq_in,
    q_sem, s_send, s_recv, p_send, p_recv, t_send, t_recv, h_send, h_recv,
):
    me = lax.axis_index("ctx")
    hd = lax.axis_index("head")
    x, y = me // SIDE, me % SIDE

    def device(o, du, dv):
        dx, dy = (du, dv) if o == 0 else (dv, du)
        return ((x + dx + 2 * SIDE) % SIDE) * SIDE + (y + dy + 2 * SIDE) % SIDE

    def copy(src, dst, send, recv, target):
        return pltpu.make_async_remote_copy(
            src_ref=src, dst_ref=dst, send_sem=send, recv_sem=recv,
            device_id={"ctx": target}, device_id_type=MESH,
        )

    q_copy = pltpu.make_async_copy(q_hbm, q_ref, q_sem)
    q_copy.start()
    barrier = pltpu.get_barrier_semaphore()
    for o in range(2):
        for d in range(1, SIDE):
            pl.semaphore_signal(
                barrier, inc=1, device_id={"ctx": device(o, d, 0)}, device_id_type=MESH
            )
    for d in range(1, NHEAD):
        pl.semaphore_signal(
            barrier, inc=1, device_id={"head": (hd + d) % NHEAD}, device_id_type=MESH
        )
    pl.semaphore_wait(barrier, 2 * (SIDE - 1) + NHEAD - 1)

    def pick_copy(o, d):
        i = o * 3 + d - 1
        return copy(pickrows, pk_in.at[o, d - 1], p_send.at[i], p_recv.at[i], device(o, 0, -d))

    def hop(b, h, i):
        part = HALF // 2
        src, dst, du, dv = [
            (kv.at[b, :, h], near.at[b, h, 0], 1, 0),
            (kv.at[b, :, h], near.at[b, h, 2], -1, 0),
            (near.at[b, h, 0, :, 0:part], near.at[b, h, 1, :, 0:part], 1, 0),
            (near.at[b, h, 2, :, part:HALF], near.at[b, h, 1, :, part:HALF], -1, 0),
            (packed.at[b, h, 0], far.at[b, h, 0], 0, 1),
            (packed.at[b, h, 2], far.at[b, h, 2], 0, -1),
            (packed.at[b, h, 1, 0:2], relay.at[b, h, 0], 0, 1),
            (packed.at[b, h, 1, 2:4], relay.at[b, h, 1], 0, -1),
            (relay.at[b, h, 0], far.at[b, h, 1, 0:2], 0, 1),
            (relay.at[b, h, 1], far.at[b, h, 1, 2:4], 0, -1),
        ][i]
        return copy(src, dst, s_send.at[b, h, i], s_recv.at[b, h, i], device(h, du, dv))

    def start(b, *which):
        for i in which:
            for h in range(2):
                hop(b, h, i).start()

    def arrived(b, *which):
        for i in which:
            for h in range(2):
                hop(b, h, i).wait_recv()

    start(0, 0, 1)
    start(1, 0, 1)

    lane16 = lax.broadcasted_iota(jnp.int32, (NCTX, LANES), 1)
    lane8 = lax.broadcasted_iota(jnp.int32, (8, LANES), 1)
    of3 = lax.broadcasted_iota(jnp.int32, (NCTX, TOPK), 0) * QBS
    mine = lax.broadcasted_iota(jnp.int32, (8, TOPK), 0) + me * QBS
    for b in range(NSEQ):
        pick = jnp.zeros((NCTX, 1), F32)
        away = jnp.zeros((NCTX, LANES), F32)
        home = jnp.zeros((8, LANES), F32)
        for qb in range(QBS):
            entry = lists[b, qb : qb + 1, :]
            off = jnp.broadcast_to(entry, (NCTX, TOPK)) - of3
            hit = (off >= 0) & (off < QBS)
            named = jnp.max(jnp.where(hit, 1.0, 0.0), axis=1, keepdims=True)
            pick = jnp.maximum(
                pick, jnp.max(jnp.where(hit, off, 0).astype(F32), axis=1, keepdims=True)
            )
            away = jnp.where((lane16 == HD + qb) & (named < 0.5), NEG, away)
            held = jnp.broadcast_to(entry, (8, TOPK)) == mine
            named = jnp.max(jnp.where(held, 1.0, 0.0), axis=1, keepdims=True)
            home = jnp.where((lane8 == HD + qb) & (named < 0.5), NEG, home)
        bias_ref[b, 0:NCTX] = away
        bias_ref[b, NCTX : NCTX + 8] = home
        pickrows[b * NCTX : (b + 1) * NCTX] = jnp.broadcast_to(pick, (NCTX, LANES))
    for o in range(2):
        for d in range(1, SIDE):
            pick_copy(o, d).start()

    row96 = lax.broadcasted_iota(jnp.int32, (BLK, HD), 0)
    lane = lax.broadcasted_iota(jnp.int32, (BLK, TAIL), 1)
    row = lax.broadcasted_iota(jnp.int32, (BLK, TAIL), 0)
    zeros = jnp.zeros((BLK, TAIL), BF)
    ones = jnp.ones((BLK, TAIL), BF)

    def own_block(b, k, left, right):
        return jnp.concatenate([kv[b, k, 0, :, left:right], kv[b, k, 1, :, left:right]], axis=0)

    def summary(b, carry):
        first = starts[b]
        for k in range(QBS):
            at = slice(k * BLK, (k + 1) * BLK)
            live = row96 + (me * QBS + k) * BLK >= first
            for g in range(2):
                key = own_block(b, k, 2 * g * HD, (2 * g + 1) * HD)
                f = jnp.where(live, feature(key), 0.0).astype(BF)
                fk[b, g, at, :] = jnp.concatenate([f, zeros], axis=1)
                v = own_block(b, k, (2 * g + 1) * HD, (2 * g + 2) * HD)
                vown[b, g, at, :] = jnp.concatenate([v, ones], axis=1)
        for g in range(2):
            t = dot(fk[b, g], vown[b, g], TN)
            st_own[b, g] = t[:HD].astype(BF)
        return carry

    lax.fori_loop(0, NSEQ, summary, 0)

    def state_copy(o, i):
        own, got = (st_row, st_x) if o == 0 else (st_own, st_y)
        part = NSEQ // 2
        src, dst, du = [
            (own, got.at[0], 1),
            (own, got.at[2], -1),
            (got.at[0, 0:part], got.at[1, 0:part], 1),
            (got.at[2, part:NSEQ], got.at[1, part:NSEQ], -1),
        ][i]
        return copy(src, dst, t_send.at[o, i], t_recv.at[o, i], device(o, du, 0))

    def pass_on(b):
        arrived(b, 0, 1)
        start(b, 2, 3)

    def relay_on(b):
        arrived(b, 6, 7)
        start(b, 8, 9)

    def source(o, du, dv):
        return device(o, -du, -dv)

    def choose(table, at, blocks):
        w = jnp.broadcast_to(table[pl.ds(at, 1), :], (HALF, LANES)).astype(BF)
        m0, m1 = w == 0.0, w == 1.0
        out = []
        for c in range(KVW // LANES):
            b0, b1, b2 = [blocks[k, :, c * LANES : (c + 1) * LANES] for k in range(QBS)]
            out.append(jnp.where(m0, b0, jnp.where(m1, b1, b2)))
        return jnp.concatenate(out, axis=1)

    def pack(b):
        arrived(b, 2, 3)
        for h in range(2):
            for dv in range(1, SIDE):
                for du in range(SIDE):
                    blocks = kv.at[b, :, h] if du == 0 else near.at[b, h, du - 1]
                    packed[b, h, dv - 1, du] = choose(
                        pk_in.at[h, dv - 1], b * NCTX + source(h, du, 0), blocks
                    )
        start(b, 6, 7, 4, 5)

    for i in (0, 1):
        state_copy(1, i).start()
    pass_on(0)
    pass_on(1)
    for i in (0, 1):
        state_copy(1, i).wait_recv()
    for i in (2, 3):
        state_copy(1, i).start()
    for o in range(2):
        for d in range(1, SIDE):
            pick_copy(o, d).wait_recv()
    pack(0)
    for i in (2, 3):
        state_copy(1, i).wait_recv()

    def rows_sum(b, carry):
        for g in range(2):
            total = st_own[b, g].astype(F32)
            before = jnp.zeros((HD, LANES), F32)
            for d in range(1, SIDE):
                part = st_y[d - 1, b, g].astype(F32)
                total = total + part
                before = before + jnp.where(y >= d, part, 0.0)
            st_row[b, g] = total.astype(BF)
            prior[b, g] = before
        return carry

    lax.fori_loop(0, NSEQ, rows_sum, 0)
    for i in (0, 1):
        state_copy(0, i).start()
    start(2, 0, 1)
    pack(1)
    start(3, 0, 1)
    relay_on(0)
    for i in (0, 1):
        state_copy(0, i).wait_recv()
    for i in (2, 3):
        state_copy(0, i).start()
    pass_on(2)
    q_copy.wait()
    for i in (2, 3):
        state_copy(0, i).wait_recv()

    def add_x(b, carry):
        for g in range(2):
            before = prior[b, g]
            for d in range(1, SIDE):
                before = before + jnp.where(x >= d, st_x[d - 1, b, g].astype(F32), 0.0)
            prior[b, g] = before
        return carry

    lax.fori_loop(0, NSEQ, add_x, 0)

    trow = lax.broadcasted_iota(jnp.int32, (ROWS, BLK), 0) % BLK
    tlane = lax.broadcasted_iota(jnp.int32, (ROWS, BLK), 1)
    causal = trow >= tlane

    def live_rows(b, qb):
        r = lax.broadcasted_iota(jnp.int32, (ROWS, 1), 0) % BLK
        return r + (me * QBS + qb) * BLK >= starts[b]

    def linear(b):
        for g in range(2):
            state = jnp.concatenate([prior[b, g], jnp.zeros((TAIL, LANES), F32)], axis=0)
            for qb in range(QBS):
                marks = jnp.where((lane == qb) | (lane == QBS), 1.0, 0.0).astype(BF)
                base = (g * QBS + qb) * ROWS
                for h in range(GROUP):
                    c = (g * GROUP + h) * HD
                    piece = q_ref[b, qb * BLK : (qb + 1) * BLK, c : c + HD]
                    fq[qb % 2, h * BLK : (h + 1) * BLK, :] = jnp.concatenate(
                        [feature(piece).astype(BF), zeros], axis=1
                    )
                    qx[base + h * BLK : base + (h + 1) * BLK, :] = jnp.concatenate(
                        [piece, marks], axis=1
                    )
                fqv = fq[qb % 2]
                fkv = fk[b, g, qb * BLK : (qb + 1) * BLK, :]
                vo = vown[b, g, qb * BLK : (qb + 1) * BLK, :]
                inner = jnp.where(causal, dot(fqv, fkv, NT), 0.0).astype(BF)
                high = state.astype(BF)
                low = (state - high.astype(F32)).astype(BF)
                lin = dot(inner, vo, NN) + dot(fqv, high, NN) + dot(fqv, low, NN)
                if qb < QBS - 1:
                    state = state + dot(fkv, vo, TN)
                den = jnp.where(live_rows(b, qb), lin[:, HD : HD + 1], 1.0)
                lin_ref[g * QBS + qb] = lin * (1.0 / den)

    def place(first, count, load, bias):
        at = slice(first, first + count)
        for g in range(2):
            k = load(2 * g * HD, (2 * g + 1) * HD)
            v = load((2 * g + 1) * HD, (2 * g + 2) * HD)
            kx[g, at, :] = jnp.concatenate([k, bias], axis=1)
            vx[g, at, :] = jnp.concatenate([v, ones[:count]], axis=1)

    def tail_bias(b, slot_row, pos):
        listed = bias_ref[b, pl.ds(slot_row, 1), HD:LANES]
        late = jnp.where((lane == QBS) & (row.astype(F32) + pos < starts[b].astype(F32)), NEG, 0.0)
        return (listed + late).astype(BF)

    def scores(i):
        g, qb = i // QBS, i % QBS
        q = qx[i * ROWS : (i + 1) * ROWS, :]
        top = None
        for c in range(NCH):
            at = slice(c * 2 * BLK, (c + 1) * 2 * BLK)
            s = dot(q, kx[g, at, :], NT)
            parts = []
            for n in range(2):
                k = 2 * c + n - OWN0
                part = s[:, n * BLK : (n + 1) * BLK]
                if k == qb:
                    part = jnp.where(causal, part, NEG)
                parts.append(part)
                sc[i % 2, :, (2 * c + n) * BLK : (2 * c + n + 1) * BLK] = part
            t = jnp.maximum(parts[0], parts[1])
            top = t if top is None else jnp.maximum(top, t)
        mx[i % 2] = top

    def weigh(b, i):
        g, qb = i // QBS, i % QBS
        peak = jnp.max(mx[i % 2], axis=1, keepdims=True)
        for c in range(NCH):
            at = slice(c * 2 * BLK, (c + 1) * 2 * BLK)
            pw[i % 2, :, at] = jnp.exp2((sc[i % 2, :, at] - peak) * SCALE).astype(BF)
        acc = dot(pw[i % 2], vx[g], NN)
        both = lin_ref[i] + acc * (1.0 / acc[:, HD : HD + 1])
        both = jnp.where(live_rows(b, qb), both, 0.0)
        comb[b, qb * BLK : (qb + 1) * BLK, g * GROUP * HD : (g + 1) * GROUP * HD] = (
            jnp.concatenate([both[h * BLK : (h + 1) * BLK, :HD] for h in range(GROUP)], axis=1)
        )

    def attend(b, carry):
        linear(b)
        arrived(b, 4, 5, 8, 9)
        slot = 0
        for dx in range(SIDE):
            for dy in range(SIDE):
                if dx == 0 and dy == 0:
                    continue
                s = source(0, dx, dy)
                at = b * NCTX + s
                pos = (pickrows[pl.ds(at, 1), HD:LANES] + (s * QBS).astype(F32)) * BLK
                tb = tail_bias(b, s, pos)
                for h in range(2):
                    du, dv = (dx, dy) if h == 0 else (dy, dx)
                    if dv == 0:
                        whole = choose(pickrows, at, near.at[b, h, du - 1])
                    else:
                        whole = far[b, h, dv - 1, du]
                    place(
                        slot * BLK + h * HALF, HALF, lambda l, r, w=whole: w[:, l:r],
                        tb[h * HALF : (h + 1) * HALF],
                    )
                slot += 1
        for k in range(QBS):
            pos = ((me * QBS + k) * BLK).astype(F32)
            tb = tail_bias(b, NCTX + k, pos)
            place(slot * BLK, BLK, lambda l, r, k=k: own_block(b, k, l, r), tb)
            slot += 1
        scores(0)
        for i in range(QBS):
            if i + 1 < QBS:
                scores(i + 1)
            weigh(b, i)

        for c in range(NSEQ - 1):

            @pl.when(b == c)
            def _(c=c):
                relay_on(c + 1)
                if c + 2 < NSEQ:
                    pack(c + 2)
                if c == 0:
                    pass_on(3)

        scores(QBS)
        for i in range(QBS, 2 * QBS):
            if i + 1 < 2 * QBS:
                scores(i + 1)
            weigh(b, i)
        for qb in range(QBS):
            c = comb[b, qb * BLK : (qb + 1) * BLK, :]
            c2 = c * c
            high = c2.astype(BF)
            low = (c2 - high.astype(F32)).astype(BF)
            e = jnp.ones((8, WIDTH), BF)
            sq[b * QBS + qb] = dot(e, high, NT) + dot(e, low, NT)
        return carry

    lax.fori_loop(0, NSEQ, attend, 0)

    def sq_copy(d):
        return pltpu.make_async_remote_copy(
            src_ref=sq, dst_ref=sq_in.at[d - 1], send_sem=h_send.at[d - 1],
            recv_sem=h_recv.at[d - 1], device_id={"head": (hd + d) % NHEAD}, device_id_type=MESH,
        )

    for d in range(1, NHEAD):
        sq_copy(d).start()
    for d in range(1, NHEAD):
        sq_copy(d).wait_recv()

    eye = lax.broadcasted_iota(jnp.int32, (BLK, BLK), 0) == lax.broadcasted_iota(
        jnp.int32, (BLK, BLK), 1
    )
    scale_by = gain[...].astype(F32).reshape(1, WIDTH)

    def finish(n, carry):
        total = sq[n, 0:1, :]
        for d in range(1, NHEAD):
            total = total + sq_in[d - 1, n, 0:1, :]
        r = lax.rsqrt(total / (WIDTH * NHEAD) + epsilon)
        col = jnp.sum(jnp.where(eye, jnp.broadcast_to(r, (BLK, BLK)), 0.0), axis=1, keepdims=True)
        b, qb = n // QBS, n % QBS
        at = pl.ds(pl.multiple_of(qb * BLK, BLK), BLK)
        out_ref[b, at, :] = (comb[b, at, :] * col * scale_by).astype(BF)
        return carry

    lax.fori_loop(0, NSEQ * QBS, finish, 0)

    for d in range(1, NHEAD):
        sq_copy(d).wait_send()
    for o in range(2):
        for d in range(1, SIDE):
            pick_copy(o, d).wait_send()
        for i in range(4):
            state_copy(o, i).wait_send()
    for b in range(NSEQ):
        for h in range(2):
            for i in range(10):
                hop(b, h, i).wait_send()


def on_device(queries, keys_values, block_lists, starts, norm_gain):
    smem = pl.BlockSpec(memory_space=pltpu.SMEM)
    vmem = pl.BlockSpec(memory_space=pltpu.VMEM)
    dma = pltpu.SemaphoreType.DMA
    return pl.pallas_call(
        kernel,
        in_specs=[smem, vmem, pl.BlockSpec(memory_space=pl.ANY), vmem, vmem],
        out_specs=vmem,
        out_shape=jax.ShapeDtypeStruct((NSEQ, LEN, WIDTH), BF),
        scratch_shapes=[
            pltpu.VMEM((NSEQ, LEN, WIDTH), BF),
            pltpu.VMEM((NSEQ, 2, 3, QBS, HALF, KVW), BF),
            pltpu.VMEM((NSEQ, 2, 3, SIDE, HALF, KVW), BF),
            pltpu.VMEM((NSEQ, 2, 3, SIDE, HALF, KVW), BF),
            pltpu.VMEM((NSEQ, 2, 2, 2, HALF, KVW), BF),
            pltpu.VMEM((NSEQ, NCTX + 8, LANES), F32),
            pltpu.VMEM((NSEQ * NCTX, LANES), F32),
            pltpu.VMEM((2, 3, NSEQ * NCTX, LANES), F32),
            pltpu.VMEM((NSEQ, 2, HD, LANES), BF),
            pltpu.VMEM((3, NSEQ, 2, HD, LANES), BF),
            pltpu.VMEM((NSEQ, 2, HD, LANES), BF),
            pltpu.VMEM((3, NSEQ, 2, HD, LANES), BF),
            pltpu.VMEM((NSEQ, 2, HD, LANES), F32),
            pltpu.VMEM((NSEQ, 2, LEN, LANES), BF),
            pltpu.VMEM((NSEQ, 2, LEN, LANES), BF),
            pltpu.VMEM((2 * QBS, ROWS, LANES), F32),
            pltpu.VMEM((NSEQ, LEN, WIDTH), F32),
            pltpu.VMEM((2, SLOTS * BLK, LANES), BF),
            pltpu.VMEM((2, SLOTS * BLK, LANES), BF),
            pltpu.VMEM((2 * QBS * ROWS, LANES), BF),
            pltpu.VMEM((2, ROWS, LANES), BF),
            pltpu.VMEM((2, ROWS, SLOTS * BLK), F32),
            pltpu.VMEM((2, ROWS, SLOTS * BLK), BF),
            pltpu.VMEM((2, ROWS, LANES), F32),
            pltpu.VMEM((NSEQ * QBS, 8, LANES), F32),
            pltpu.VMEM((NHEAD - 1, NSEQ * QBS, 8, LANES), F32),
            dma,
            dma((NSEQ, 2, 10)),
            dma((NSEQ, 2, 10)),
            dma((6,)),
            dma((6,)),
            dma((2, 4)),
            dma((2, 4)),
            dma((NHEAD - 1,)),
            dma((NHEAD - 1,)),
        ],
        compiler_params=pltpu.CompilerParams(
            vmem_limit_bytes=60 << 20, collective_id=0, has_side_effects=True
        ),
    )(
        starts,
        block_lists,
        queries,
        keys_values.reshape(NSEQ, QBS, 2, HALF, KVW),
        norm_gain,
    )


def solution(mesh):
    return jax.shard_map(
        on_device,
        mesh=mesh,
        in_specs=(
            P(None, "ctx", "head"),
            P(None, "ctx", "head"),
            P(None, "ctx", None),
            P(),
            P("head"),
        ),
        out_specs=P(None, "ctx", "head"),
        check_vma=False,
    )
```

time: 124 us -> 117 us (0.944)
  Pallas kernels: 115 us -> 112 us
  other arithmetic: 2.05 us -> 0 us
  local copies, waits for them, and re-layouts: 6.38 us -> 4.51 us
    pallas_call x1, Pallas kernels: 115 us -> 112 us  [on_device(): pl.pallas_call(kernel, in_specs=[smem, vmem, pl.BlockSpec(memory_space=pl...]
    unnamed x3 -> x2, local copies, waits for them, and re-layouts: 3.23 us -> 4.51 us
    reshape x1 -> x0, local copies, waits for them, and re-layouts: 1.28 us -> none  [on_device(): norm_gain.reshape(1, WIDTH)]
where the time goes in v3:
time: 117 us
  Pallas kernels  112 us (96%)
  local copies, waits for them, and re-layouts  4.51 us (4%)
    pallas_call x1, Pallas kernels, on_device(): pl.pallas_call(kernel, in_specs=[smem, vmem, pl.BlockSpec(memory_space=pl...  112 us
    unnamed x2, local copies, waits for them, and re-layouts  4.51 us

profile of v3, /device:TPU:1, one launch (start us, length us, event | category | flops | bytes accessed | tf_op | source)
XLA Modules:
  0.0 116.9 jit_solution(2042079551645157489)
XLA Ops:
  0.0 1.3 %copy.6.lists = s32[4,3,16]{2,1,0:T(4,128)} copy(s32[4,3,16]{2,0,1:T(4,128)} %param.7) | data formatting | bytes 1536 | tf_op args[2]
  1.3 112.3 %shard_map.55 = bf16[4,384,768]{2,1,0:T(8,128)(2,1)} custom-call(s32[4]{0:T(128)} %starts.1, s32[4,3,16]{2,1,0:T(4,128)} %copy.6.lists, bf16[4,384,768]{2,1,0:T(8,128)(2,1)} %q_hbm.1, bf16[4,3,2,64,384]{4,3,2,1,0:T(8,128)(2,1)} %bitcast.1, bf16[768]{0:T(1024)(128)(2,1)} %gain.1), custom_call_target="tpu_custom_call" | custom-call | tf_op jit(solution)/shard_map/pallas_call | solution.py:451
  113.6 3.2 %copy.8 = bf16[4,384,768]{2,1,0:T(8,128)(2,1)} copy(bf16[4,384,768]{2,1,0:T(8,128)(2,1)} %shard_map.55) | data formatting | bytes 4718592

commit v4 on v3

--- a/solution.py
+++ b/solution.py
@@ -47,10 +47,10 @@
 
 
 def kernel(
-    starts, lists, q_hbm, kv, gain, out_ref,
-    q_ref, near, packed, far, relay, bias_ref, pickrows, pk_in, st_own, st_y, st_row, st_x,
+    starts, lists, q_hbm, kv, gain, out_hbm,
+    q_ref, near, packed, far, relay, bias_ref, pickrows, pickpack, pk_raw, pk_in, st_own, st_y, st_row, st_x,
     prior, fk, vown, lin_ref, comb, kx, vx, qx, fq, sc, pw, mx, sq, sq_in,
-    q_sem, s_send, s_recv, p_send, p_recv, t_send, t_recv, h_send, h_recv,
+    out_ref, out_sem, q_sem, s_send, s_recv, p_send, p_recv, t_send, t_recv, h_send, h_recv,
 ):
     me = lax.axis_index("ctx")
     hd = lax.axis_index("head")
@@ -82,7 +82,7 @@
 
     def pick_copy(o, d):
         i = o * 3 + d - 1
-        return copy(pickrows, pk_in.at[o, d - 1], p_send.at[i], p_recv.at[i], device(o, 0, -d))
+        return copy(pickpack, pk_raw.at[o, d - 1], p_send.at[i], p_recv.at[i], device(o, 0, -d))
 
     def hop(b, h, i):
         part = HALF // 2
@@ -115,6 +115,9 @@
 
     lane16 = lax.broadcasted_iota(jnp.int32, (NCTX, LANES), 1)
     lane8 = lax.broadcasted_iota(jnp.int32, (8, LANES), 1)
+    match = lane16 == lax.broadcasted_iota(jnp.int32, (NCTX, LANES), 0)
+    pickpack[...] = jnp.zeros((8, LANES), F32)
+    sq[...] = jnp.zeros((16, LANES), F32)
     of3 = lax.broadcasted_iota(jnp.int32, (NCTX, TOPK), 0) * QBS
     mine = lax.broadcasted_iota(jnp.int32, (8, TOPK), 0) + me * QBS
     for b in range(NSEQ):
@@ -135,7 +138,9 @@
             home = jnp.where((lane8 == HD + qb) & (named < 0.5), NEG, home)
         bias_ref[b, 0:NCTX] = away
         bias_ref[b, NCTX : NCTX + 8] = home
-        pickrows[b * NCTX : (b + 1) * NCTX] = jnp.broadcast_to(pick, (NCTX, LANES))
+        spread = jnp.broadcast_to(pick, (NCTX, LANES))
+        pickrows[b * NCTX : (b + 1) * NCTX] = spread
+        pickpack[b : b + 1, :] = jnp.sum(jnp.where(match, spread, 0.0), axis=0, keepdims=True)
     for o in range(2):
         for d in range(1, SIDE):
             pick_copy(o, d).start()
@@ -220,6 +225,10 @@
     for o in range(2):
         for d in range(1, SIDE):
             pick_copy(o, d).wait_recv()
+            for b in range(NSEQ):
+                line = jnp.broadcast_to(pk_raw[o, d - 1, b : b + 1, :], (NCTX, LANES))
+                col = jnp.sum(jnp.where(match, line, 0.0), axis=1, keepdims=True)
+                pk_in[o, d - 1, b * NCTX : (b + 1) * NCTX] = jnp.broadcast_to(col, (NCTX, LANES))
     pack(0)
     for i in (2, 3):
         state_copy(1, i).wait_recv()
@@ -397,7 +406,7 @@
             high = c2.astype(BF)
             low = (c2 - high.astype(F32)).astype(BF)
             e = jnp.ones((8, WIDTH), BF)
-            sq[b * QBS + qb] = dot(e, high, NT) + dot(e, low, NT)
+            sq[pl.ds(b * QBS + qb, 1), :] = (dot(e, high, NT) + dot(e, low, NT))[0:1]
         return carry
 
     lax.fori_loop(0, NSEQ, attend, 0)
@@ -418,18 +427,25 @@
     )
     scale_by = gain[...].astype(F32).reshape(1, WIDTH)
 
+    def out_copy(n):
+        rows = pl.ds(pl.multiple_of(n % QBS * BLK, BLK), BLK) if not isinstance(n, int) else pl.ds(n % QBS * BLK, BLK)
+        return pltpu.make_async_copy(out_ref.at[n], out_hbm.at[n // QBS, rows], out_sem.at[n])
+
     def finish(n, carry):
-        total = sq[n, 0:1, :]
+        total = sq[pl.ds(n, 1), :]
         for d in range(1, NHEAD):
-            total = total + sq_in[d - 1, n, 0:1, :]
+            total = total + sq_in[d - 1, pl.ds(n, 1), :]
         r = lax.rsqrt(total / (WIDTH * NHEAD) + epsilon)
         col = jnp.sum(jnp.where(eye, jnp.broadcast_to(r, (BLK, BLK)), 0.0), axis=1, keepdims=True)
         b, qb = n // QBS, n % QBS
         at = pl.ds(pl.multiple_of(qb * BLK, BLK), BLK)
-        out_ref[b, at, :] = (comb[b, at, :] * col * scale_by).astype(BF)
+        out_ref[n] = (comb[b, at, :] * col * scale_by).astype(BF)
+        out_copy(n).start()
         return carry
 
     lax.fori_loop(0, NSEQ * QBS, finish, 0)
+    for n in range(NSEQ * QBS):
+        out_copy(n).wait()
 
     for d in range(1, NHEAD):
         sq_copy(d).wait_send()
@@ -451,7 +467,7 @@
     return pl.pallas_call(
         kernel,
         in_specs=[smem, vmem, pl.BlockSpec(memory_space=pl.ANY), vmem, vmem],
-        out_specs=vmem,
+        out_specs=pl.BlockSpec(memory_space=pl.ANY),
         out_shape=jax.ShapeDtypeStruct((NSEQ, LEN, WIDTH), BF),
         scratch_shapes=[
             pltpu.VMEM((NSEQ, LEN, WIDTH), BF),
@@ -461,6 +477,8 @@
             pltpu.VMEM((NSEQ, 2, 2, 2, HALF, KVW), BF),
             pltpu.VMEM((NSEQ, NCTX + 8, LANES), F32),
             pltpu.VMEM((NSEQ * NCTX, LANES), F32),
+            pltpu.VMEM((8, LANES), F32),
+            pltpu.VMEM((2, 3, 8, LANES), F32),
             pltpu.VMEM((2, 3, NSEQ * NCTX, LANES), F32),
             pltpu.VMEM((NSEQ, 2, HD, LANES), BF),
             pltpu.VMEM((3, NSEQ, 2, HD, LANES), BF),
@@ -478,8 +496,10 @@
             pltpu.VMEM((2, ROWS, SLOTS * BLK), F32),
             pltpu.VMEM((2, ROWS, SLOTS * BLK), BF),
             pltpu.VMEM((2, ROWS, LANES), F32),
-            pltpu.VMEM((NSEQ * QBS, 8, LANES), F32),
-            pltpu.VMEM((NHEAD - 1, NSEQ * QBS, 8, LANES), F32),
+            pltpu.VMEM((16, LANES), F32),
+            pltpu.VMEM((NHEAD - 1, 16, LANES), F32),
+            pltpu.VMEM((NSEQ * QBS, BLK, WIDTH), BF),
+            dma((NSEQ * QBS,)),
             dma,
             dma((NSEQ, 2, 10)),
             dma((NSEQ, 2, 10)),

time: 117 us -> 114 us (0.974)
  Pallas kernels: 112 us -> 109 us
    pallas_call x1, Pallas kernels: 112 us -> 109 us  [on_device(): pl.pallas_call(kernel, in_specs=[smem, vmem, pl.BlockSpec(memory_space=pl...]
where the time goes in v4:
time: 114 us
  Pallas kernels  109 us (96%)
  local copies, waits for them, and re-layouts  4.51 us (4%)
    pallas_call x1, Pallas kernels, on_device(): pl.pallas_call(kernel, in_specs=[smem, vmem, pl.BlockSpec(memory_space=pl...  109 us
    unnamed x2, local copies, waits for them, and re-layouts  4.51 us

profile of v4, /device:TPU:1, one launch (start us, length us, event | category | flops | bytes accessed | tf_op | source)
XLA Modules:
  0.0 113.7 jit_solution(5745765520273887558)
XLA Ops:
  0.0 1.3 %copy.6.lists = s32[4,3,16]{2,1,0:T(4,128)} copy(s32[4,3,16]{2,0,1:T(4,128)} %param.7) | data formatting | bytes 1536 | tf_op args[2]
  1.3 109.2 %shard_map.55 = bf16[4,384,768]{2,1,0:T(8,128)(2,1)} custom-call(s32[4]{0:T(128)} %starts.1, s32[4,3,16]{2,1,0:T(4,128)} %copy.6.lists, bf16[4,384,768]{2,1,0:T(8,128)(2,1)} %q_hbm.1, bf16[4,3,2,64,384]{4,3,2,1,0:T(8,128)(2,1)} %bitcast.1, bf16[768]{0:T(1024)(128)(2,1)} %gain.1), custom_call_target="tpu_custom_call" | custom-call | tf_op jit(solution)/shard_map/pallas_call | solution.py:467
  110.5 3.2 %copy.8 = bf16[4,384,768]{2,1,0:T(8,128)(2,1)} copy(bf16[4,384,768]{2,1,0:T(8,128)(2,1)} %shard_map.55) | data formatting | bytes 4718592

commit v5 on v4

--- a/solution.py
+++ b/solution.py
@@ -354,6 +354,16 @@
     def attend(b, carry):
         linear(b)
         arrived(b, 4, 5, 8, 9)
+        for c in range(NSEQ - 1):
+
+            @pl.when(b == c)
+            def _(c=c):
+                relay_on(c + 1)
+                if c + 2 < NSEQ:
+                    pack(c + 2)
+                if c == 0:
+                    pass_on(3)
+
         slot = 0
         for dx in range(SIDE):
             for dy in range(SIDE):
@@ -380,23 +390,7 @@
             place(slot * BLK, BLK, lambda l, r, k=k: own_block(b, k, l, r), tb)
             slot += 1
         scores(0)
-        for i in range(QBS):
-            if i + 1 < QBS:
-                scores(i + 1)
-            weigh(b, i)
-
-        for c in range(NSEQ - 1):
-
-            @pl.when(b == c)
-            def _(c=c):
-                relay_on(c + 1)
-                if c + 2 < NSEQ:
-                    pack(c + 2)
-                if c == 0:
-                    pass_on(3)
-
-        scores(QBS)
-        for i in range(QBS, 2 * QBS):
+        for i in range(2 * QBS):
             if i + 1 < 2 * QBS:
                 scores(i + 1)
             weigh(b, i)

time: 114 us -> 112 us (0.982)
    pallas_call x1, Pallas kernels: 109 us -> 108 us  [on_device(): pl.pallas_call(kernel, in_specs=[smem, vmem, pl.BlockSpec(memory_space=pl...]
where the time goes in v5:
time: 112 us
  Pallas kernels  108 us (96%)
  local copies, waits for them, and re-layouts  4.51 us (4%)
    pallas_call x1, Pallas kernels, on_device(): pl.pallas_call(kernel, in_specs=[smem, vmem, pl.BlockSpec(memory_space=pl...  108 us
    unnamed x2, local copies, waits for them, and re-layouts  4.51 us

profile of v5, /device:TPU:1, one launch (start us, length us, event | category | flops | bytes accessed | tf_op | source)
XLA Modules:
  0.0 112.2 jit_solution(13871080113949848916)
XLA Ops:
  0.0 1.3 %copy.6.lists = s32[4,3,16]{2,1,0:T(4,128)} copy(s32[4,3,16]{2,0,1:T(4,128)} %param.7) | data formatting | bytes 1536 | tf_op args[2]
  1.3 107.7 %shard_map.55 = bf16[4,384,768]{2,1,0:T(8,128)(2,1)} custom-call(s32[4]{0:T(128)} %starts.1, s32[4,3,16]{2,1,0:T(4,128)} %copy.6.lists, bf16[4,384,768]{2,1,0:T(8,128)(2,1)} %q_hbm.1, bf16[4,3,2,64,384]{4,3,2,1,0:T(8,128)(2,1)} %bitcast.1, bf16[768]{0:T(1024)(128)(2,1)} %gain.1), custom_call_target="tpu_custom_call" | custom-call | tf_op jit(solution)/shard_map/pallas_call | solution.py:461
  109.0 3.2 %copy.8 = bf16[4,384,768]{2,1,0:T(8,128)(2,1)} copy(bf16[4,384,768]{2,1,0:T(8,128)(2,1)} %shard_map.55) | data formatting | bytes 4718592
